TPU v7x, 32 devices: a whole 2x2x4 slice. The times are simulated.
32 devices in a mesh: scen: 8 (over y, x, core), col: 4 (over z).
Axes of the slice: x: 2, y: 2, z: 4, core: 2. Of those that a mesh axis runs over, the one named last changes fastest.
Arguments:
- inverses: float32 [8, 1024, 1024], P('scen'), as said below
- coupling: float32 [8, 1024, 4096], P('scen', None, 'col'), may hold values from -0.1875 to 0.1875
- tile_mask: int32 [8, 8], P('scen'), may hold values 0 or 1
- hess_diag: float32 [512], replicated, may hold values from 1 to 16
Outputs:
- factor: float32 [4096, 512], P(('col', 'scen'))
Inputs may be any that keep to these rules, and one draw needn't show every extreme that they name: `inverses`: each scenario's matrix is symmetric and positive definite.
All inputs are finite; a program needn't handle non-finite values. No bound on the sum of `tile_mask` on one device may be relied on, other than what follows from the above.
Results may differ from a plain program's by a relative error of at most 0.0001.
Values sent between devices are 32-bit elements; how exact they have to be, the bound alone decides.
No kernel may reach another device: no remote copies, remote signals or barrier semaphores. Data moves between devices by JAX's collectives and lax.ppermute only.
A program may use at most 64 MiB of HBM per device.

v0:
```python
import functools

import jax
import jax.numpy as jnp
from jax import lax
from jax.experimental import pallas as pl
from jax.experimental.pallas import tpu as pltpu
from jax.sharding import PartitionSpec as P


BLOCK = 128
SUB = 8


def high(left, right, dims):
    return lax.dot_general(
        left, right, (dims, ((), ())), precision=lax.Precision.HIGH, preferred_element_type=jnp.float32
    )


def full(left, right, dims):
    return lax.dot_general(
        left, right, (dims, ((), ())), precision=lax.Precision.HIGHEST, preferred_element_type=jnp.float32
    )


def eliminate(tiles):
    count, size = len(tiles), tiles[0].shape[1]
    lane = lax.broadcasted_iota(jnp.int32, (SUB, size), 1)
    sub = lax.broadcasted_iota(jnp.int32, (SUB, size), 0)

    def lanes(x, c):
        return jnp.broadcast_to(x[:, c : c + 1], (SUB, size))

    def subs(x, q):
        return jnp.broadcast_to(x[q : q + 1, :], (SUB, size))

    def row_times(columns, upper, inverse):
        raw, times = [], []
        for q in range(SUB):
            value = columns[q]
            for p in range(q):
                value = value - times[p] * upper[p, q]
            raw.append(value)
            times.append(value * inverse[q])
        return raw, times

    scaled, scales, ready = [], [], None
    for at in range(count):
        low = SUB * at
        rows = tiles[at]
        cols = ready or [lanes(rows, low + q) for q in range(SUB)]
        if at + 1 < count:
            ready = [lanes(tiles[at + 1], low + SUB + q) for q in range(SUB)]
            below = [lanes(tiles[at + 1], low + q) for q in range(SUB)]
        inverse, upper, pivots, factors = [], {}, None, []
        for q in range(SUB):
            pivot = subs(cols[q], q)
            pivots = pivot if pivots is None else jnp.where(sub == q, pivot, pivots)
            inverse.append(1.0 / pivot)
            factors.append(jnp.where(sub > q, cols[q] * inverse[q], 0.0))
            for p in range(q + 1, SUB):
                upper[q, p] = subs(cols[q], p)
                cols[p] = cols[p] - factors[q] * upper[q, p]
        if at + 1 < count:
            raw, next_times = row_times(below, upper, inverse)
            for q in range(SUB):
                for p in range(SUB):
                    ready[q] = ready[q] - next_times[p] * subs(raw[p], q)
        for q in range(SUB):
            pivot_row = jnp.where(lane == low + q, 1.0, subs(rows, q))
            rows = jnp.where((lane == low + q) & (sub > q), 0.0, rows) - factors[q] * pivot_row
        pivot_rows = []
        for q in range(SUB):
            row = jnp.where(lane == low + q, 1.0, subs(rows, q))
            pivot_rows.append(jnp.where((lane > low + q) & (lane < low + SUB), 0.0, row))
        own = (lane >= low) & (lane < low + SUB)
        for other in range(at + 1, count):
            if other == at + 1:
                times = next_times
            else:
                _, times = row_times([lanes(tiles[other], low + q) for q in range(SUB)], upper, inverse)
            tile = jnp.where(own, 0.0, tiles[other])
            for q in range(SUB):
                tile = tile - times[q] * pivot_rows[q]
            tiles[other] = tile
        scale = lax.rsqrt(pivots)
        scales.append(scale)
        scaled.append(rows * scale)
    return scaled, scales


def vmem(count):
    return [pl.BlockSpec(memory_space=pltpu.VMEM)] * count


SMEM = pl.BlockSpec(memory_space=pltpu.SMEM)


def shape(*sizes):
    return jax.ShapeDtypeStruct(sizes, jnp.float32)


def strips(nb):
    for i in range(nb // 2):
        yield i, nb - 1 - i, 0
        yield i, i, (nb - i) * BLOCK


HBM = pl.BlockSpec(memory_space=pltpu.HBM)


def split(x):
    high_part = x.astype(jnp.bfloat16)
    return high_part, (x - high_part.astype(jnp.float32)).astype(jnp.bfloat16)


def three(left, right, dims):
    def one(a, b):
        return lax.dot_general(a, b, (dims, ((), ())), preferred_element_type=jnp.float32)

    (ah, al), (bh, bl) = left, right
    return one(ah, bh) + (one(ah, bl) + one(al, bh))


def product_kernel(edges, tall, place_ref, mask_ref, inverse_hbm, coupling_hbm, *refs):
    count = len(edges) - 1
    pieces = refs[:count]
    keep_a, keep_b, send, panel, rows, ph, plo, qh, ql, rect, values, sems, out_sems = refs[count:]

    @pl.when(place_ref[0] == 0)
    def _():
        depth, width = panel.shape
        nb, steps, tile = width // BLOCK, depth // tall, depth // mask_ref.shape[1]
        copies = [pltpu.make_async_copy(coupling_hbm.at[:, pl.ds(0, width)], panel, sems.at[0])]
        for i in range(steps):
            copies.append(pltpu.make_async_copy(inverse_hbm.at[pl.ds(i * tall, tall)], rows.at[i], sems.at[1 + i]))
        for copy in copies:
            copy.start()
        stores = []
        kept = [mask_ref[0, t].astype(jnp.float32) for t in range(depth // tile)]
        copies[0].wait()
        for t in range(depth // tile):
            here = slice(t * tile, (t + 1) * tile)
            ph[here, :], plo[here, :] = split(panel[here, :] * kept[t])
        for i in range(steps):
            copies[1 + i].wait()
            value = three(split(rows[i]), (ph[...], plo[...]), ((1,), (0,)))
            for t in range(i * tall // tile, (i + 1) * tall // tile):
                part = value[t * tile - i * tall : (t + 1) * tile - i * tall, :] * kept[t]
                here = slice(t * tile, (t + 1) * tile)
                qh[here, :], ql[here, :] = split(part)
                values[here, :] = part
            for k in range(count):
                if i * tall < edges[k + 1] <= (i + 1) * tall:
                    mine = pl.ds(edges[k], edges[k + 1] - edges[k])
                    stores.append(pltpu.make_async_copy(values.at[mine], pieces[k], out_sems.at[k]))
                    stores[-1].start()
        for i, block, low in strips(nb):
            wide = (block + 1) * BLOCK
            mine = slice(block * BLOCK, wide)
            rect[i * BLOCK : (i + 1) * BLOCK, low : low + wide] = three(
                (ph[:, mine], plo[:, mine]), (qh[:, :wide], ql[:, :wide]), ((0,), (0,))
            )
        half = rect.shape[0] // 2
        core = place_ref[1] & 1
        mine = pl.multiple_of(core * half, half)
        theirs = pl.multiple_of((1 - core) * half, half)
        keep_a[...] = rect[pl.ds(mine, half // 2), :]
        keep_b[...] = rect[pl.ds(mine + half // 2, half // 2), :]
        send[...] = rect[pl.ds(theirs, half), :]
        for store in stores:
            store.wait()


def product(place, mask, inverse, coupling, width, edges):
    depth, count = inverse.shape[0], len(edges) - 1
    nb, tall = width // BLOCK, depth // 4
    high_rows, wide = nb // 2 * BLOCK, (nb + 1) * BLOCK
    return pl.pallas_call(
        functools.partial(product_kernel, edges, tall),
        out_shape=tuple(shape(b - a, width) for a, b in zip(edges, edges[1:]))
        + (shape(high_rows // 4, wide), shape(high_rows // 4, wide), shape(high_rows // 2, wide)),
        in_specs=[SMEM, SMEM, HBM, HBM],
        out_specs=tuple([HBM] * count + vmem(3)),
        scratch_shapes=[pltpu.VMEM((depth, width), jnp.float32), pltpu.VMEM((depth // tall, tall, depth), jnp.float32)]
        + [pltpu.VMEM((depth, width), jnp.bfloat16)] * 4
        + [pltpu.VMEM((high_rows, wide), jnp.float32), pltpu.VMEM((depth, width), jnp.float32)]
        + [pltpu.SemaphoreType.DMA((1 + depth // tall,)), pltpu.SemaphoreType.DMA((count,))],
        compiler_params=pltpu.CompilerParams(vmem_limit_bytes=61 << 20),
        cost_estimate=pl.CostEstimate(
            flops=6 * depth * width * (depth + width), bytes_accessed=4 * depth * (depth + 2 * width), transcendentals=0
        ),
    )(place, mask, inverse, coupling)


def collect_kernel(planes, count, place_ref, *refs):
    groups, (out_ref, sems) = refs[: planes * count], refs[planes * count :]
    for h in range(planes):

        @pl.when(place_ref[0] == h)
        def _(h=h):
            low, copies = 0, []
            for k in range(count):
                ref = groups[h * count + k]
                copies.append(pltpu.make_async_copy(ref, out_ref.at[pl.ds(low, ref.shape[0])], sems.at[k]))
                low += ref.shape[0]
            for copy in copies:
                copy.start()
            for copy in copies:
                copy.wait()


def collect(place, groups):
    count = len(groups[0])
    rows, width = sum(x.shape[0] for x in groups[0]), groups[0][0].shape[1]
    return pl.pallas_call(
        functools.partial(collect_kernel, len(groups), count),
        out_shape=shape(rows, width),
        in_specs=[SMEM] + [pl.BlockSpec(memory_space=pl.ANY)] * (len(groups) * count),
        out_specs=vmem(1)[0],
        scratch_shapes=[pltpu.SemaphoreType.DMA((count,))],
        compiler_params=pltpu.CompilerParams(vmem_limit_bytes=8 << 20),
        cost_estimate=pl.CostEstimate(flops=0, bytes_accessed=8 * rows * width, transcendentals=0),
    )(place, *[x for group in groups for x in group])


def part_kernel(planes, place_ref, first_ref, local_hbm, *refs):
    pieces, (keep_ref, send_ref, piece_ref, local_ref, sems) = refs[:planes], refs[planes:]
    late, wide = piece_ref.shape[0], keep_ref.shape[2]
    depth = local_hbm.shape[0]
    bring = pltpu.make_async_copy(local_hbm.at[pl.ds(depth - late, late)], local_ref, sems.at[0])
    bring.start()
    for h in range(planes):

        @pl.when(place_ref[0] == h)
        def _(h=h):
            copy = pltpu.make_async_copy(pieces[h], piece_ref, sems.at[1])
            copy.start()
            copy.wait()

    bring.wait()
    core = place_ref[1] & 1
    left = split(piece_ref[...])
    for ref, bit in ((send_ref, 1 - core), (keep_ref, core)):
        for j in range(ref.shape[0]):
            here = pl.ds(pl.multiple_of((2 * j + bit) * wide, wide), wide)
            ref[j] = first_ref[:, here] + three(left, split(local_ref[:, here]), ((0,), (0,)))


def part(place, first, local, pieces, scen):
    width, cols = first.shape
    late = pieces[0].shape[0]
    half = shape(scen // 2, width, cols // scen)
    return pl.pallas_call(
        functools.partial(part_kernel, len(pieces)),
        out_shape=(half, half),
        in_specs=[SMEM] + vmem(1) + [HBM] + [pl.BlockSpec(memory_space=pl.ANY)] * len(pieces),
        out_specs=tuple(vmem(2)),
        scratch_shapes=[
            pltpu.VMEM((late, width), jnp.float32),
            pltpu.VMEM((late, cols), jnp.float32),
            pltpu.SemaphoreType.DMA((2,)),
        ],
        compiler_params=pltpu.CompilerParams(vmem_limit_bytes=16 << 20),
        cost_estimate=pl.CostEstimate(flops=6 * late * width * cols, bytes_accessed=8 * width * cols, transcendentals=0),
    )(place, first, local, *pieces)


def turn_kernel(cuts, place_ref, own_ref, got_ref, *outs):
    for (low, high_row, position, bit), keep_ref, send_ref in zip(cuts, outs[::2], outs[1::2]):
        mine = (place_ref[1] >> bit) & 1
        rows = slice(low, high_row)
        for ref, value in ((keep_ref, mine), (send_ref, 1 - mine)):
            for j in range(ref.shape[0]):
                at = ((j >> position) << (position + 1)) + (j & ((1 << position) - 1)) + (value << position)
                ref[j] = own_ref[at, rows, :] + got_ref[at, rows, :]


def turn(place, own, got, cuts):
    blocks, _, wide = own.shape
    outs = tuple(shape(blocks // 2, high_row - low, wide) for low, high_row, _, _ in cuts for _ in range(2))
    return pl.pallas_call(
        functools.partial(turn_kernel, cuts),
        out_shape=outs,
        in_specs=[SMEM] + vmem(2),
        out_specs=tuple(vmem(len(outs))),
        compiler_params=pltpu.CompilerParams(vmem_limit_bytes=12 << 20),
        cost_estimate=pl.CostEstimate(flops=own.size, bytes_accessed=12 * own.size, transcendentals=0),
    )(place, own, got)


def factor_kernel(place_ref, own_a, own_b, other_a, other_b, diag_ref, own_ref, piece_ref, l_ref, w_ref, rect_ref, base_ref, scale_ref):
    size = w_ref.shape[0]
    nb = size // BLOCK
    plane, me = place_ref[0], place_ref[1]

    @pl.when(plane == 0)
    def _():
        half = rect_ref.shape[0] // 2
        quarter = half // 2
        core = me & 1
        mine = pl.multiple_of(core * half, half)
        theirs = pl.multiple_of((1 - core) * half, half)
        rect_ref[pl.ds(mine, quarter), :] = own_a[...]
        rect_ref[pl.ds(mine + quarter, quarter), :] = own_b[...]
        rect_ref[pl.ds(theirs, quarter), :] = other_a[...]
        rect_ref[pl.ds(theirs + quarter, quarter), :] = other_b[...]
        row = lax.broadcasted_iota(jnp.int32, (BLOCK, BLOCK), 0)
        col = lax.broadcasted_iota(jnp.int32, (BLOCK, BLOCK), 1)
        for i, block, low in strips(nb):
            here = slice(block * BLOCK, (block + 1) * BLOCK)
            for k in range(block + 1):
                there = slice(k * BLOCK, (k + 1) * BLOCK)
                part = rect_ref[i * BLOCK : (i + 1) * BLOCK, low + k * BLOCK : low + (k + 1) * BLOCK]
                if k == block:
                    part = jnp.where(col <= row, part, part.T)
                    part = part + jnp.where(col == row, diag_ref[:, here], 0.0)
                w_ref[here, there] = part

        def nt(left, right):
            return full(left, right, ((1,), (1,)))

        def nn(left, right):
            return full(left, right, ((1,), (0,)))

        for j in range(nb):
            low, top = j * BLOCK, (j + 1) * BLOCK
            mine = slice(low, top)
            scaled, scales = eliminate([w_ref[low + SUB * t : low + SUB * (t + 1), mine] for t in range(BLOCK // SUB)])
            for t in range(BLOCK // SUB):
                base_ref[SUB * t : SUB * t + SUB, :] = scaled[t]
                scale_ref[SUB * t : SUB * t + SUB, :] = scales[t]
            both = base_ref[...]
            inverse = jnp.where(col < row, both, jnp.where(col == row, scale_ref[...], 0.0))
            l_ref[mine, mine] = jnp.where(col >= row, both, 0.0).T
            if top < size:
                l_ref[mine, top:] = jnp.zeros((BLOCK, size - top), jnp.float32)
            if j:
                w_ref[mine, :low] = nn(inverse, w_ref[mine, :low])
            w_ref[mine, mine] = inverse
            if top < size:
                panel = nt(w_ref[top:, mine], inverse)
                l_ref[top:, mine] = panel
                for k in range(j + 1, nb):
                    here, skip = slice(k * BLOCK, (k + 1) * BLOCK), (k - j - 1) * BLOCK
                    w_ref[k * BLOCK :, here] = w_ref[k * BLOCK :, here] - nt(panel[skip:], panel[skip : skip + BLOCK])
                if j:
                    w_ref[top:, :low] = w_ref[top:, :low] - nn(panel, w_ref[mine, :low])
                w_ref[top:, mine] = -nn(panel, inverse)
        for i, block, low in strips(nb):
            for k in range(block + 1):
                rect_ref[i * BLOCK : (i + 1) * BLOCK, low + k * BLOCK : low + (k + 1) * BLOCK] = w_ref[
                    block * BLOCK : (block + 1) * BLOCK, k * BLOCK : (k + 1) * BLOCK
                ]
        rows = own_ref.shape[0]
        first = jnp.minimum(place_ref[2], size - rows)
        own_ref[...] = l_ref[pl.ds(pl.multiple_of(first, rows), rows), :]
        each = piece_ref.shape[0]
        piece_ref[...] = rect_ref[pl.ds(pl.multiple_of(me * each, each), each), :]


def factor(place, parts, diag, each, rows):
    size = diag.shape[1]
    nb = size // BLOCK
    tall, wide = nb // 2 * BLOCK, (nb + 1) * BLOCK
    return pl.pallas_call(
        factor_kernel,
        out_shape=(shape(rows, size), shape(each, wide)),
        in_specs=[SMEM] + vmem(5),
        out_specs=tuple(vmem(2)),
        scratch_shapes=[
            pltpu.VMEM((size, size), jnp.float32),
            pltpu.VMEM((size, size), jnp.float32),
            pltpu.VMEM((tall, wide), jnp.float32),
            pltpu.VMEM((BLOCK, BLOCK), jnp.float32),
            pltpu.VMEM((BLOCK, BLOCK), jnp.float32),
        ],
        compiler_params=pltpu.CompilerParams(vmem_limit_bytes=16 << 20),
        cost_estimate=pl.CostEstimate(flops=20 * size**3, bytes_accessed=12 * size * size, transcendentals=size),
    )(place, *parts, diag)


def last_kernel(count, place_ref, *refs):
    pieces, (keep_a, got_a, keep_b, got_b, own_ref, out_ref, rect_ref, rows_ref) = refs[:count], refs[count:]
    me, first = place_ref[1], place_ref[2]
    rows, width = out_ref.shape
    nb = width // BLOCK
    each = pieces[0].shape[0]
    if len(keep_a.shape) == 3:
        half = keep_a.shape[1]
        rows_ref[:, :half] = (keep_a[0] + got_a[0]).T
        rows_ref[:, half:] = (keep_b[0] + got_b[0]).T
    else:
        half = rows // 2
        rows_ref[:half, :] = keep_a[...] + got_a[...]
        rows_ref[half:, :] = keep_b[...] + got_b[...]
    for m in range(count):
        rect_ref[pl.ds(pl.multiple_of((me ^ m) * each, each), each), :] = pieces[m][...]
    for i, block, low in strips(nb):
        wide = (block + 1) * BLOCK
        part = rect_ref[i * BLOCK : (i + 1) * BLOCK, low : low + wide]
        part = jnp.concatenate(
            [part[:, : wide - BLOCK], jnp.where(
                lax.broadcasted_iota(jnp.int32, (BLOCK, BLOCK), 1) <= lax.broadcasted_iota(jnp.int32, (BLOCK, BLOCK), 0),
                part[:, wide - BLOCK :], 0.0)], axis=1) if wide > BLOCK else part
        out_ref[:, block * BLOCK : (block + 1) * BLOCK] = three(split(rows_ref[:, :wide]), split(part), ((1,), (1,)))

    @pl.when(first < width)
    def _():
        out_ref[...] = own_ref[...]


def last(place, pieces, sums, own):
    rows, width = own.shape
    nb = width // BLOCK
    tall, wide = nb // 2 * BLOCK, (nb + 1) * BLOCK
    return pl.pallas_call(
        functools.partial(last_kernel, len(pieces)),
        out_shape=shape(rows, width),
        in_specs=[SMEM] + vmem(len(pieces) + 5),
        out_specs=vmem(1)[0],
        scratch_shapes=[pltpu.VMEM((tall, wide), jnp.float32), pltpu.VMEM((rows, width), jnp.float32)],
        compiler_params=pltpu.CompilerParams(vmem_limit_bytes=12 << 20),
        cost_estimate=pl.CostEstimate(flops=6 * rows * width * width, bytes_accessed=8 * width * width, transcendentals=0),
    )(place, *pieces, *sums, own)


def hop(x, source, target):
    return lax.ppermute(x, "col", [(source, target)])


def exchange(x, mask, count):
    return lax.ppermute(x, "scen", [(i, i ^ mask) for i in range(count)])


def orders(count):
    bits = count.bit_length() - 1
    split = 1 + bits // 2
    return bits, list(range(1, split)), list(range(split, bits))


def halve(x, names, bit, count):
    axis = names.index(bit)
    mine = (lax.axis_index("scen") >> bit) & 1
    keep = lax.dynamic_index_in_dim(x, mine, axis, keepdims=False)
    send = lax.dynamic_index_in_dim(x, 1 - mine, axis, keepdims=False)
    return keep, exchange(send, 1 << bit, count), [n for n in names if n != bit]


def scatter_sum(x):
    count = lax.axis_size("scen")
    bits, first, second = orders(count)
    rows = x.shape[0] // count
    x = x.reshape((2,) * bits + (rows,) + x.shape[1:])
    keep, got, names = halve(x, list(range(bits - 1, -1, -1)), 0, count)
    x = keep + got
    lead = (slice(None),) * len(names)
    parts = [x[lead + (slice(0, rows // 2),)], x[lead + (slice(rows // 2, rows),)]]
    lists, pairs = [names, names], [None, None]
    for a, b in zip(first + second, second + first):
        for i, bit in ((0, a), (1, b)):
            if pairs[i] is not None:
                parts[i] = pairs[i][0] + pairs[i][1]
            keep, got, lists[i] = halve(parts[i], lists[i], bit, count)
            pairs[i] = (keep, got)
    return pairs[0] + pairs[1]


def scatter_sum_columns(place, first, local, pieces):
    count = lax.axis_size("scen")
    bits, near, far = orders(count)
    half = first.shape[0] // 2
    keep, send = part(place, first, local, pieces, count)
    got = exchange(send, 1, count)
    left = [list(range(1, bits)), list(range(1, bits))]
    pairs = None
    for a, b in zip(near + far, far + near):
        if pairs is None:
            cuts = tuple((i * half, (i + 1) * half, left[i].index(bit), bit) for i, bit in ((0, a), (1, b)))
            outs = turn(place, keep, got, cuts)
        else:
            outs = ()
            for i, bit in ((0, a), (1, b)):
                outs += turn(place, *pairs[i], ((0, half, left[i].index(bit), bit),))
        pairs = []
        for i, bit in ((0, a), (1, b)):
            left[i].remove(bit)
            pairs.append((outs[2 * i], exchange(outs[2 * i + 1], 1 << bit, count)))
    return pairs[0] + pairs[1]


PIECES = 8
LATE = 1


def bounds(depth):
    units = depth // (2 * SUB)
    return [units * k // PIECES * 2 * SUB for k in range(PIECES + 1)]


def program(inverses, coupling, tile_mask, hess_diag):
    local = coupling[0]
    width = hess_diag.shape[0]
    scen, planes = lax.axis_size("scen"), lax.axis_size("col")
    me, plane = lax.axis_index("scen").astype(jnp.int32), lax.axis_index("col").astype(jnp.int32)
    rows = local.shape[1] // scen
    place = jnp.stack([plane, me, plane * local.shape[1] + me * rows])
    edge = bounds(local.shape[0])

    *own, keep_a, keep_b, send = product(place, tile_mask, inverses[0], local, width, edge)

    groups = [own]
    for h in range(planes - 1):
        groups.append([hop(groups[h][k], h, h + 1) for k in range(PIECES)])

    got = exchange(send, 1, scen)
    a, b = keep_a + got[: got.shape[0] // 2], keep_b + got[got.shape[0] // 2 :]
    _, near, far = orders(scen)
    for p, q in zip(near + far, far + near):
        got_a = exchange(a, 1 << p, scen)
        got_b = exchange(b, 1 << q, scen)
        a, b = a + got_a, b + got_b
    parts = (a, b, exchange(a, 1, scen), exchange(b, 1, scen))
    each = width // BLOCK // 2 * BLOCK // scen
    lower, piece = factor(place, parts, hess_diag[None, :], each, rows)

    mine = jnp.where(plane == 0, piece, 0.0)
    for h in range(1, planes):
        piece = hop(piece, h - 1, h)
        mine = mine + piece
    pieces = [mine if m == 0 else exchange(mine, m, scen) for m in range(0, scen, 2)]
    pieces = [p for m in range(0, scen, 2) for p in (pieces[m // 2], exchange(pieces[m // 2], 1, scen))]

    cut = PIECES - LATE
    early = edge[cut]
    top = collect(place, [group[:cut] for group in groups])
    if rows % BLOCK == 0:
        first = high(top, local[:early], ((0,), (0,)))
        sums = scatter_sum_columns(place, first, local, [group[cut] for group in groups])
    else:
        bottom = collect(place, [group[cut:] for group in groups])
        first, second = high(local[:early], top, ((0,), (0,))), high(local[early:], bottom, ((0,), (0,)))
        sums = scatter_sum(first + second)
    return last(place, pieces, sums, lower)


def solution(mesh):
    in_specs = (P("scen", None, None), P("scen", None, "col"), P("scen", None), P())
    out_specs = P(("col", "scen"), None)
    return jax.shard_map(program, mesh=mesh, in_specs=in_specs, out_specs=out_specs, check_vma=False)
```

profile of v0, /device:TPU:16, one launch (start us, length us, event | category | flops | bytes accessed | tf_op | source)
XLA Modules:
  0.0 160.1 jit_solution(7133681499053644003)
XLA Ops:
  0.6 1.7 %shard_map.46 = (f32[128,512]{1,0:T(8,128)}, f32[128,512]{1,0:T(8,128)}, f32[128,512]{1,0:T(8,128)}, f32[128,512]{1,0:T(8,128)}, f32[128,512]{1,0:T(8,128)}, /*i...) custom-call(s32[3]{0:T(128)} %pad_add_fusion.place_ref, ...), custom_call_target="tpu_custom_call" | custom-call | flops 4831838208 | bytes 8388608 | tf_op jit(solution)/shard_map/pallas_call | solution.py:180
  14.4 28.1 %collective-permute-done.24.refs_14_ = f32[128,512]{1,0:T(8,128)S(1)} collective-permute-done((f32[128,512]{1,0:T(8,128)S(1)}, f32[128,512]{1,0:T(8,128)S(1)}, u32[]{:S(2)}, u32[]{:S(2)}) %collective-permute-start.24) | collective-permute-done | bytes 262176 | tf_op jit(solution)/shard_map/ppermute | solution.py:430
  43.7 4.3 %collective-permute-done.25.refs_15_ = f32[128,512]{1,0:T(8,128)S(1)} collective-permute-done((f32[128,512]{1,0:T(8,128)S(1)}, f32[128,512]{1,0:T(8,128)S(1)}, u32[]{:S(2)}, u32[]{:S(2)}) %collective-permute-start.25) | collective-permute-done | bytes 262176 | tf_op jit(solution)/shard_map/ppermute | solution.py:430
  49.3 4.3 %collective-permute-done.26.refs_16_ = f32[128,512]{1,0:T(8,128)S(1)} collective-permute-done((f32[128,512]{1,0:T(8,128)S(1)}, f32[128,512]{1,0:T(8,128)S(1)}, u32[]{:S(2)}, u32[]{:S(2)}) %collective-permute-start.26) | collective-permute-done | bytes 262176 | tf_op jit(solution)/shard_map/ppermute | solution.py:430
  55.0 4.3 %collective-permute-done.27.refs_17_ = f32[128,512]{1,0:T(8,128)S(1)} collective-permute-done((f32[128,512]{1,0:T(8,128)S(1)}, f32[128,512]{1,0:T(8,128)S(1)}, u32[]{:S(2)}, u32[]{:S(2)}) %collective-permute-start.27) | collective-permute-done | bytes 262176 | tf_op jit(solution)/shard_map/ppermute | solution.py:430
  60.6 5.1 %collective-permute-done.28.refs_18_ = f32[128,512]{1,0:T(8,128)S(1)} collective-permute-done((f32[128,512]{1,0:T(8,128)S(1)}, f32[128,512]{1,0:T(8,128)S(1)}, u32[]{:S(2)}, u32[]{:S(2)}) %collective-permute-start.28) | collective-permute-done | bytes 262176 | tf_op jit(solution)/shard_map/ppermute | solution.py:430
  67.0 4.3 %collective-permute-done.29.refs_19_ = f32[128,512]{1,0:T(8,128)S(1)} collective-permute-done((f32[128,512]{1,0:T(8,128)S(1)}, f32[128,512]{1,0:T(8,128)S(1)}, u32[]{:S(2)}, u32[]{:S(2)}) %collective-permute-start.29) | collective-permute-done | bytes 262176 | tf_op jit(solution)/shard_map/ppermute | solution.py:430
  72.6 4.3 %collective-permute-done.30.refs_20_ = f32[128,512]{1,0:T(8,128)S(1)} collective-permute-done((f32[128,512]{1,0:T(8,128)S(1)}, f32[128,512]{1,0:T(8,128)S(1)}, u32[]{:S(2)}, u32[]{:S(2)}) %collective-permute-start.30) | collective-permute-done | bytes 262176 | tf_op jit(solution)/shard_map/ppermute | solution.py:430
  78.2 3.5 %collective-permute-done.39.refs_2_ = f32[128,512]{1,0:T(8,128)S(1)} collective-permute-done((f32[128,512]{1,0:T(8,128)S(1)}, f32[128,512]{1,0:T(8,128)S(1)}, u32[]{:S(2)}, u32[]{:S(2)}) %collective-permute-start.39) | collective-permute-done | bytes 262176 | tf_op jit(solution)/shard_map/ppermute | solution.py:430
  85.8 1.6 collective-permute-start.40
  87.4 2.3 %collective-permute-done.35.refs_25_ = f32[128,512]{1,0:T(8,128)S(1)} collective-permute-done((f32[128,512]{1,0:T(8,128)S(1)}, f32[128,512]{1,0:T(8,128)S(1)}, u32[]{:S(2)}, u32[]{:S(2)}) %collective-permute-start.35) | collective-permute-done | bytes 262176 | tf_op jit(solution)/shard_map/ppermute | solution.py:430
  89.7 5.6 %collective-permute-done.36.refs_26_ = f32[128,512]{1,0:T(8,128)S(1)} collective-permute-done((f32[128,512]{1,0:T(8,128)S(1)}, f32[128,512]{1,0:T(8,128)S(1)}, u32[]{:S(2)}, u32[]{:S(2)}) %collective-permute-start.36) | collective-permute-done | bytes 262176 | tf_op jit(solution)/shard_map/ppermute | solution.py:430
  95.3 5.6 %collective-permute-done.37.refs_27_ = f32[128,512]{1,0:T(8,128)S(1)} collective-permute-done((f32[128,512]{1,0:T(8,128)S(1)}, f32[128,512]{1,0:T(8,128)S(1)}, u32[]{:S(2)}, u32[]{:S(2)}) %collective-permute-start.37) | collective-permute-done | bytes 262176 | tf_op jit(solution)/shard_map/ppermute | solution.py:430
  108.4 3.7 %fusion.first_ref = f32[512,1024]{1,0:T(8,128)S(1)} fusion(f32[896,512]{1,0:T(8,128)S(1)} %shard_map.48, f32[1,1024,1024]{2,1,0:T(8,128)S(1)} %copy-done), kind=kOutput, calls=%fused_computation | convolution fusion | flops 2818572288 | bytes 7602176 | tf_op jit(solution)/shard_map/dot_general | solution.py:16
  112.2 1.7 %shard_map.49 = (f32[4,512,128]{2,1,0:T(8,128)S(1)}, f32[4,512,128]{2,1,0:T(8,128)S(1)}) custom-call(s32[3]{0:T(128)S(1)} %copy-done.9, f32[512,1024]{1,0:T(8,128)S(1)} %fusion.first_ref, f32[1024,1024]{1,0:T(8,128)S(1)} %bitcast.11, f32[128,512]{1,0:T(8,128)S(1)} %copy-done.8, f32[128,512]{1,0:T(8,128)S(1)} %collective-permute-done.38.refs_1_, ...), custom_call_target="tpu_custom_call" | custom-call | flops 402653184 | bytes 4194304 | tf_op jit(solution)/shard_map/pallas_call | solution.py:255
  114.0 1.8 %collective-permute-start.3 = (f32[64,640]{1,0:T(8,128)S(1)}, f32[64,640]{1,0:T(8,128)S(1)}, u32[]{:S(2)}, u32[]{:S(2)}) collective-permute-start(f32[64,640]{1,0:T(8,128)S(1)} %get-tuple-element.51), channel_id=1, source_target_pairs={{0,16},{4,20},{8,24},{12,28},{16,0},{20,4},{24,8},{28,12},{1,17},{... | collective-permute-start | bytes 491528 | tf_op jit(solution)/shard_map/ppermute | solution.py:434
  115.8 1.4 collective-permute-start.1
  117.2 3.5 %collective-permute-done.3 = f32[64,640]{1,0:T(8,128)S(1)} collective-permute-done((f32[64,640]{1,0:T(8,128)S(1)}, f32[64,640]{1,0:T(8,128)S(1)}, u32[]{:S(2)}, u32[]{:S(2)}) %collective-permute-start.3) | collective-permute-done | bytes 163872 | tf_op jit(solution)/shard_map/ppermute | solution.py:434
  120.7 1.7 %collective-permute-start.4 = (f32[64,640]{1,0:T(8,128)S(1)}, f32[64,640]{1,0:T(8,128)S(1)}, u32[]{:S(2)}, u32[]{:S(2)}) collective-permute-start(f32[64,640]{1,0:T(8,128)S(1)} %add.35), channel_id=1, source_target_pairs={{0,8},{4,12},{8,0},{12,4},{16,24},{20,28},{24,16},{28,20},{1,9},{5... | collective-permute-start | bytes 491528 | tf_op jit(solution)/shard_map/ppermute | solution.py:434
  122.4 1.5 collective-permute-start.2
  124.0 2.5 %collective-permute-done.4 = f32[64,640]{1,0:T(8,128)S(1)} collective-permute-done((f32[64,640]{1,0:T(8,128)S(1)}, f32[64,640]{1,0:T(8,128)S(1)}, u32[]{:S(2)}, u32[]{:S(2)}) %collective-permute-start.4) | collective-permute-done | bytes 163872 | tf_op jit(solution)/shard_map/ppermute | solution.py:434
  126.6 1.4 collective-permute-done.2
  128.1 1.4 collective-permute-done.5.other_a
  132.8 5.2 %collective-permute-done.8 = f32[32,640]{1,0:T(8,128)} collective-permute-done((f32[32,640]{1,0:T(8,128)S(1)}, f32[32,640]{1,0:T(8,128)}, u32[]{:S(2)}, u32[]{:S(2)}) %collective-permute-start.8) | collective-permute-done | bytes 81952 | tf_op jit(solution)/shard_map/ppermute | solution.py:430
  138.0 1.9 %collective-permute-start.9 = (f32[32,640]{1,0:T(8,128)}, f32[32,640]{1,0:T(8,128)}, u32[]{:S(2)}, u32[]{:S(2)}) collective-permute-start(f32[32,640]{1,0:T(8,128)} %collective-permute-done.8), channel_id=1, source_target_pairs={{2,3},{6,7},{10,11},{14,15},{18,19},{22,23},{26,27},{30,31}} | collective-permute-start | bytes 245768 | tf_op jit(solution)/shard_map/ppermute | solution.py:430
  143.8 1.4 collective-permute-start.15
  145.2 1.5 collective-permute-start.13
  147.3 2.5 %collective-permute-done.42.got_ref = f32[2,256,128]{2,1,0:T(8,128)S(1)} collective-permute-done((f32[2,256,128]{2,1,0:T(8,128)S(1)}, f32[2,256,128]{2,1,0:T(8,128)S(1)}, u32[]{:S(2)}, u32[]{:S(2)}) %collective-permute-start.42) | collective-permute-done | bytes 262176 | tf_op jit(solution)/shard_map/ppermute | solution.py:434
  150.7 2.0 %collective-permute-start.43 = (f32[1,256,128]{2,1,0:T(8,128)S(1)}, f32[1,256,128]{2,1,0:T(8,128)S(1)}, u32[]{:S(2)}, u32[]{:S(2)}) collective-permute-start(f32[1,256,128]{2,1,0:T(8,128)S(1)} %get-tuple-element.45), channel_id=1, source_target_pairs={{0,16},{4,20},{8,24},{12,28},{16,0},{20,4},{24,8},{28,12},{1,17},{... | collective-permute-start | bytes 393224 | tf_op jit(solution)/shard_map/ppermute | solution.py:434
  153.3 1.4 collective-permute-start.45
  156.5 1.8 %collective-permute-done.45.refs_11_ = f32[1,256,128]{2,1,0:T(8,128)S(1)} collective-permute-done((f32[1,256,128]{2,1,0:T(8,128)S(1)}, f32[1,256,128]{2,1,0:T(8,128)S(1)}, u32[]{:S(2)}, u32[]{:S(2)}) %collective-permute-start.45) | collective-permute-done | bytes 131104 | tf_op jit(solution)/shard_map/ppermute | solution.py:434
  158.3 1.8 %shard_map.53 = f32[128,512]{1,0:T(8,128)} custom-call(s32[3]{0:T(128)S(1)} %copy-done.9, f32[32,640]{1,0:T(8,128)S(1)} %add_add_fusion.refs_0_, f32[32,640]{1,0:T(8,128)S(1)} %collective-permute-done.10.refs_1_, f32[32,640]{1,0:T(8,128)S(1)} %collective-permute-done.11.refs_2_, f32[32,640]{1,0:T(8,128)S(1)} %collective-permute-done.12.refs_3_, ...), custom_call_target="tpu_custom_call" | custom-call | flops 201326592 | bytes 2097152 | tf_op jit(solution)/shard_map/pallas_call | solution.py:418
  (104 shorter events, 44.4 us)
Async XLA Ops:
  6.4 5.3 %collective-permute-start.23 = (f32[128,512]{1,0:T(8,128)}, f32[128,512]{1,0:T(8,128)S(1)}, u32[]{:S(2)}, u32[]{:S(2)}) collective-permute-start(f32[128,512]{1,0:T(8,128)} %get-tuple-element.38.refs_6_), channel_id=1, source_target_pairs={{0,1},{4,5},{8,9},{12,13},{16,17},{20,21},{24,25},{28,29}} | collective-permute-start | bytes 786440 | tf_op jit(solution)/shard_map/ppermute | solution.py:430
  7.1 5.9 %collective-permute-start.38 = (f32[128,512]{1,0:T(8,128)}, f32[128,512]{1,0:T(8,128)S(1)}, u32[]{:S(2)}, u32[]{:S(2)}) collective-permute-start(f32[128,512]{1,0:T(8,128)} %get-tuple-element.39.refs_0_), channel_id=1, source_target_pairs={{0,1},{4,5},{8,9},{12,13},{16,17},{20,21},{24,25},{28,29}} | collective-permute-start | bytes 786440 | tf_op jit(solution)/shard_map/ppermute | solution.py:430
  7.8 34.6 %collective-permute-start.24 = (f32[128,512]{1,0:T(8,128)S(1)}, f32[128,512]{1,0:T(8,128)S(1)}, u32[]{:S(2)}, u32[]{:S(2)}) collective-permute-start(f32[128,512]{1,0:T(8,128)S(1)} %collective-permute-done.17.refs_7_), channel_id=1, source_target_pairs={{1,2},{5,6},{9,10},{13,14},{17,18},{21,22},{25,26},{29,30}} | collective-permute-start | bytes 786440 | tf_op jit(solution)/shard_map/ppermute | solution.py:430
  9.2 38.9 %collective-permute-start.25 = (f32[128,512]{1,0:T(8,128)S(1)}, f32[128,512]{1,0:T(8,128)S(1)}, u32[]{:S(2)}, u32[]{:S(2)}) collective-permute-start(f32[128,512]{1,0:T(8,128)S(1)} %collective-permute-done.18.refs_8_), channel_id=1, source_target_pairs={{1,2},{5,6},{9,10},{13,14},{17,18},{21,22},{25,26},{29,30}} | collective-permute-start | bytes 786440 | tf_op jit(solution)/shard_map/ppermute | solution.py:430
  10.5 43.2 %collective-permute-start.26 = (f32[128,512]{1,0:T(8,128)S(1)}, f32[128,512]{1,0:T(8,128)S(1)}, u32[]{:S(2)}, u32[]{:S(2)}) collective-permute-start(f32[128,512]{1,0:T(8,128)S(1)} %collective-permute-done.19.refs_9_), channel_id=1, source_target_pairs={{1,2},{5,6},{9,10},{13,14},{17,18},{21,22},{25,26},{29,30}} | collective-permute-start | bytes 786440 | tf_op jit(solution)/shard_map/ppermute | solution.py:430
  11.8 47.5 %collective-permute-start.27 = (f32[128,512]{1,0:T(8,128)S(1)}, f32[128,512]{1,0:T(8,128)S(1)}, u32[]{:S(2)}, u32[]{:S(2)}) collective-permute-start(f32[128,512]{1,0:T(8,128)S(1)} %collective-permute-done.20.refs_10_), channel_id=1, source_target_pairs={{1,2},{5,6},{9,10},{13,14},{17,18},{21,22},{25,26},{29,30}} | collective-permute-start | bytes 786440 | tf_op jit(solution)/shard_map/ppermute | solution.py:430
  13.1 52.6 %collective-permute-start.28 = (f32[128,512]{1,0:T(8,128)S(1)}, f32[128,512]{1,0:T(8,128)S(1)}, u32[]{:S(2)}, u32[]{:S(2)}) collective-permute-start(f32[128,512]{1,0:T(8,128)S(1)} %collective-permute-done.21.refs_11_), channel_id=1, source_target_pairs={{1,2},{5,6},{9,10},{13,14},{17,18},{21,22},{25,26},{29,30}} | collective-permute-start | bytes 786440 | tf_op jit(solution)/shard_map/ppermute | solution.py:430
  42.4 28.9 %collective-permute-start.29 = (f32[128,512]{1,0:T(8,128)S(1)}, f32[128,512]{1,0:T(8,128)S(1)}, u32[]{:S(2)}, u32[]{:S(2)}) collective-permute-start(f32[128,512]{1,0:T(8,128)S(1)} %collective-permute-done.22.refs_12_), channel_id=1, source_target_pairs={{1,2},{5,6},{9,10},{13,14},{17,18},{21,22},{25,26},{29,30}} | collective-permute-start | bytes 786440 | tf_op jit(solution)/shard_map/ppermute | solution.py:430
  48.1 28.9 %collective-permute-start.30 = (f32[128,512]{1,0:T(8,128)S(1)}, f32[128,512]{1,0:T(8,128)S(1)}, u32[]{:S(2)}, u32[]{:S(2)}) collective-permute-start(f32[128,512]{1,0:T(8,128)S(1)} %collective-permute-done.23.refs_13_), channel_id=1, source_target_pairs={{1,2},{5,6},{9,10},{13,14},{17,18},{21,22},{25,26},{29,30}} | collective-permute-start | bytes 786440 | tf_op jit(solution)/shard_map/ppermute | solution.py:430
  53.7 28.1 %collective-permute-start.39 = (f32[128,512]{1,0:T(8,128)S(1)}, f32[128,512]{1,0:T(8,128)S(1)}, u32[]{:S(2)}, u32[]{:S(2)}) collective-permute-start(f32[128,512]{1,0:T(8,128)S(1)} %collective-permute-done.38.refs_1_), channel_id=1, source_target_pairs={{1,2},{5,6},{9,10},{13,14},{17,18},{21,22},{25,26},{29,30}} | collective-permute-start | bytes 786440 | tf_op jit(solution)/shard_map/ppermute | solution.py:430
  59.3 23.8 %collective-permute-start.31 = (f32[128,512]{1,0:T(8,128)S(1)}, f32[128,512]{1,0:T(8,128)S(1)}, u32[]{:S(2)}, u32[]{:S(2)}) collective-permute-start(f32[128,512]{1,0:T(8,128)S(1)} %collective-permute-done.24.refs_14_), channel_id=1, source_target_pairs={{2,3},{6,7},{10,11},{14,15},{18,19},{22,23},{26,27},{30,31}} | collective-permute-start | bytes 786440 | tf_op jit(solution)/shard_map/ppermute | solution.py:430
  65.7 18.7 %collective-permute-start.32 = (f32[128,512]{1,0:T(8,128)S(1)}, f32[128,512]{1,0:T(8,128)S(1)}, u32[]{:S(2)}, u32[]{:S(2)}) collective-permute-start(f32[128,512]{1,0:T(8,128)S(1)} %collective-permute-done.25.refs_15_), channel_id=1, source_target_pairs={{2,3},{6,7},{10,11},{14,15},{18,19},{22,23},{26,27},{30,31}} | collective-permute-start | bytes 786440 | tf_op jit(solution)/shard_map/ppermute | solution.py:430
  71.3 14.4 %collective-permute-start.33 = (f32[128,512]{1,0:T(8,128)S(1)}, f32[128,512]{1,0:T(8,128)S(1)}, u32[]{:S(2)}, u32[]{:S(2)}) collective-permute-start(f32[128,512]{1,0:T(8,128)S(1)} %collective-permute-done.26.refs_16_), channel_id=1, source_target_pairs={{2,3},{6,7},{10,11},{14,15},{18,19},{22,23},{26,27},{30,31}} | collective-permute-start | bytes 786440 | tf_op jit(solution)/shard_map/ppermute | solution.py:430
  76.9 8.9 %collective-permute-start.34 = (f32[128,512]{1,0:T(8,128)S(1)}, f32[128,512]{1,0:T(8,128)S(1)}, u32[]{:S(2)}, u32[]{:S(2)}) collective-permute-start(f32[128,512]{1,0:T(8,128)S(1)} %collective-permute-done.27.refs_17_), channel_id=1, source_target_pairs={{2,3},{6,7},{10,11},{14,15},{18,19},{22,23},{26,27},{30,31}} | collective-permute-start | bytes 786440 | tf_op jit(solution)/shard_map/ppermute | solution.py:430
  81.8 8.0 %collective-permute-start.35 = (f32[128,512]{1,0:T(8,128)S(1)}, f32[128,512]{1,0:T(8,128)S(1)}, u32[]{:S(2)}, u32[]{:S(2)}) collective-permute-start(f32[128,512]{1,0:T(8,128)S(1)} %collective-permute-done.28.refs_18_), channel_id=1, source_target_pairs={{2,3},{6,7},{10,11},{14,15},{18,19},{22,23},{26,27},{30,31}} | collective-permute-start | bytes 786440 | tf_op jit(solution)/shard_map/ppermute | solution.py:430
  83.1 12.3 %collective-permute-start.36 = (f32[128,512]{1,0:T(8,128)S(1)}, f32[128,512]{1,0:T(8,128)S(1)}, u32[]{:S(2)}, u32[]{:S(2)}) collective-permute-start(f32[128,512]{1,0:T(8,128)S(1)} %collective-permute-done.29.refs_19_), channel_id=1, source_target_pairs={{2,3},{6,7},{10,11},{14,15},{18,19},{22,23},{26,27},{30,31}} | collective-permute-start | bytes 786440 | tf_op jit(solution)/shard_map/ppermute | solution.py:430
  84.4 16.6 %collective-permute-start.37 = (f32[128,512]{1,0:T(8,128)S(1)}, f32[128,512]{1,0:T(8,128)S(1)}, u32[]{:S(2)}, u32[]{:S(2)}) collective-permute-start(f32[128,512]{1,0:T(8,128)S(1)} %collective-permute-done.30.refs_20_), channel_id=1, source_target_pairs={{2,3},{6,7},{10,11},{14,15},{18,19},{22,23},{26,27},{30,31}} | collective-permute-start | bytes 786440 | tf_op jit(solution)/shard_map/ppermute | solution.py:430
  85.7 28.2 %collective-permute-start = (f32[128,640]{1,0:T(8,128)}, f32[128,640]{1,0:T(8,128)S(1)}, u32[]{:S(2)}, u32[]{:S(2)}) collective-permute-start(f32[128,640]{1,0:T(8,128)} %get-tuple-element.29), channel_id=1, source_target_pairs={{0,4},{4,0},{8,12},{12,8},{16,20},{20,16},{24,28},{28,24},{1,5},{5... | collective-permute-start | bytes 983048 | tf_op jit(solution)/shard_map/ppermute | solution.py:434
  85.8 26.3 %collective-permute-start.40 = (f32[128,512]{1,0:T(8,128)S(1)}, f32[128,512]{1,0:T(8,128)S(1)}, u32[]{:S(2)}, u32[]{:S(2)}) collective-permute-start(f32[128,512]{1,0:T(8,128)S(1)} %collective-permute-done.39.refs_2_), channel_id=1, source_target_pairs={{2,3},{6,7},{10,11},{14,15},{18,19},{22,23},{26,27},{30,31}} | collective-permute-start | bytes 786440 | tf_op jit(solution)/shard_map/ppermute | solution.py:430
  113.9 26.1 %collective-permute-start.41 = (f32[4,512,128]{2,1,0:T(8,128)S(1)}, f32[4,512,128]{2,1,0:T(8,128)S(1)}, u32[]{:S(2)}, u32[]{:S(2)}) collective-permute-start(f32[4,512,128]{2,1,0:T(8,128)S(1)} %get-tuple-element.41), channel_id=1, source_target_pairs={{0,4},{4,0},{8,12},{12,8},{16,20},{20,16},{24,28},{28,24},{1,5},{5... | collective-permute-start | bytes 3145736 | tf_op jit(solution)/shard_map/ppermute | solution.py:434
  114.0 6.6 %collective-permute-start.3 = (f32[64,640]{1,0:T(8,128)S(1)}, f32[64,640]{1,0:T(8,128)S(1)}, u32[]{:S(2)}, u32[]{:S(2)}) collective-permute-start(f32[64,640]{1,0:T(8,128)S(1)} %get-tuple-element.51), channel_id=1, source_target_pairs={{0,16},{4,20},{8,24},{12,28},{16,0},{20,4},{24,8},{28,12},{1,17},{... | collective-permute-start | bytes 491528 | tf_op jit(solution)/shard_map/ppermute | solution.py:434
  115.8 6.6 %collective-permute-start.1 = (f32[64,640]{1,0:T(8,128)S(1)}, f32[64,640]{1,0:T(8,128)S(1)}, u32[]{:S(2)}, u32[]{:S(2)}) collective-permute-start(f32[64,640]{1,0:T(8,128)S(1)} %get-tuple-element.52), channel_id=1, source_target_pairs={{0,8},{4,12},{8,0},{12,4},{16,24},{20,28},{24,16},{28,20},{1,9},{5... | collective-permute-start | bytes 491528 | tf_op jit(solution)/shard_map/ppermute | solution.py:434
  120.7 5.8 %collective-permute-start.4 = (f32[64,640]{1,0:T(8,128)S(1)}, f32[64,640]{1,0:T(8,128)S(1)}, u32[]{:S(2)}, u32[]{:S(2)}) collective-permute-start(f32[64,640]{1,0:T(8,128)S(1)} %add.35), channel_id=1, source_target_pairs={{0,8},{4,12},{8,0},{12,4},{16,24},{20,28},{24,16},{28,20},{1,9},{5... | collective-permute-start | bytes 491528 | tf_op jit(solution)/shard_map/ppermute | solution.py:434
  122.4 5.5 %collective-permute-start.2 = (f32[64,640]{1,0:T(8,128)S(1)}, f32[64,640]{1,0:T(8,128)S(1)}, u32[]{:S(2)}, u32[]{:S(2)}) collective-permute-start(f32[64,640]{1,0:T(8,128)S(1)} %add.32), channel_id=1, source_target_pairs={{0,16},{4,20},{8,24},{12,28},{16,0},{20,4},{24,8},{28,12},{1,17},{... | collective-permute-start | bytes 491528 | tf_op jit(solution)/shard_map/ppermute | solution.py:434
  131.5 6.5 %collective-permute-start.8 = (f32[32,640]{1,0:T(8,128)S(1)}, f32[32,640]{1,0:T(8,128)}, u32[]{:S(2)}, u32[]{:S(2)}) collective-permute-start(f32[32,640]{1,0:T(8,128)S(1)} %collective-permute-done.7), channel_id=1, source_target_pairs={{1,2},{5,6},{9,10},{13,14},{17,18},{21,22},{25,26},{29,30}} | collective-permute-start | bytes 245768 | tf_op jit(solution)/shard_map/ppermute | solution.py:430
  140.6 9.2 %collective-permute-start.42 = (f32[2,256,128]{2,1,0:T(8,128)S(1)}, f32[2,256,128]{2,1,0:T(8,128)S(1)}, u32[]{:S(2)}, u32[]{:S(2)}) collective-permute-start(f32[2,256,128]{2,1,0:T(8,128)S(1)} %get-tuple-element.43), channel_id=1, source_target_pairs={{0,8},{4,12},{8,0},{12,4},{16,24},{20,28},{24,16},{28,20},{1,9},{5... | collective-permute-start | bytes 786440 | tf_op jit(solution)/shard_map/ppermute | solution.py:434
  141.8 9.0 %collective-permute-start.44 = (f32[2,256,128]{2,1,0:T(8,128)S(1)}, f32[2,256,128]{2,1,0:T(8,128)S(1)}, u32[]{:S(2)}, u32[]{:S(2)}) collective-permute-start(f32[2,256,128]{2,1,0:T(8,128)S(1)} %get-tuple-element.47), channel_id=1, source_target_pairs={{0,16},{4,20},{8,24},{12,28},{16,0},{20,4},{24,8},{28,12},{1,17},{... | collective-permute-start | bytes 786440 | tf_op jit(solution)/shard_map/ppermute | solution.py:434
  143.8 9.5 %collective-permute-start.15 = (f32[32,640]{1,0:T(8,128)S(1)}, f32[32,640]{1,0:T(8,128)S(1)}, u32[]{:S(2)}, u32[]{:S(2)}) collective-permute-start(f32[32,640]{1,0:T(8,128)S(1)} %add_add_fusion.refs_0_), channel_id=1, source_target_pairs={{0,24},{4,28},{8,16},{12,20},{16,8},{20,12},{24,0},{28,4},{1,25},{... | collective-permute-start | bytes 245768 | tf_op jit(solution)/shard_map/ppermute | solution.py:434
  145.2 9.5 %collective-permute-start.13 = (f32[32,640]{1,0:T(8,128)S(1)}, f32[32,640]{1,0:T(8,128)S(1)}, u32[]{:S(2)}, u32[]{:S(2)}) collective-permute-start(f32[32,640]{1,0:T(8,128)S(1)} %add_add_fusion.refs_0_), channel_id=1, source_target_pairs={{0,16},{4,20},{8,24},{12,28},{16,0},{20,4},{24,8},{28,12},{1,17},{... | collective-permute-start | bytes 245768 | tf_op jit(solution)/shard_map/ppermute | solution.py:434
  146.7 8.0 %collective-permute-start.11 = (f32[32,640]{1,0:T(8,128)S(1)}, f32[32,640]{1,0:T(8,128)S(1)}, u32[]{:S(2)}, u32[]{:S(2)}) collective-permute-start(f32[32,640]{1,0:T(8,128)S(1)} %add_add_fusion.refs_0_), channel_id=1, source_target_pairs={{0,8},{4,12},{8,0},{12,4},{16,24},{20,28},{24,16},{28,20},{1,9},{5... | collective-permute-start | bytes 245768 | tf_op jit(solution)/shard_map/ppermute | solution.py:434
  149.8 5.4 %collective-permute-start.10 = (f32[32,640]{1,0:T(8,128)S(1)}, f32[32,640]{1,0:T(8,128)S(1)}, u32[]{:S(2)}, u32[]{:S(2)}) collective-permute-start(f32[32,640]{1,0:T(8,128)S(1)} %add_add_fusion.refs_0_), channel_id=1, source_target_pairs={{0,4},{4,0},{8,12},{12,8},{16,20},{20,16},{24,28},{28,24},{1,5},{5... | collective-permute-start | bytes 245768 | tf_op jit(solution)/shard_map/ppermute | solution.py:434
  150.7 5.7 %collective-permute-start.43 = (f32[1,256,128]{2,1,0:T(8,128)S(1)}, f32[1,256,128]{2,1,0:T(8,128)S(1)}, u32[]{:S(2)}, u32[]{:S(2)}) collective-permute-start(f32[1,256,128]{2,1,0:T(8,128)S(1)} %get-tuple-element.45), channel_id=1, source_target_pairs={{0,16},{4,20},{8,24},{12,28},{16,0},{20,4},{24,8},{28,12},{1,17},{... | collective-permute-start | bytes 393224 | tf_op jit(solution)/shard_map/ppermute | solution.py:434
  (28 other events, 195.1 us)
where the time goes:
time: 161 us; the launch traced here: 160 us
  waiting for transfers between devices  91.7 us (57%)
  starting transfers between devices  46.6 us (29%)
  Pallas kernels  8.51 us (5%)
  local copies, waits for them, and re-layouts  7.31 us (5%)
  matrix products  3.71 us (2%)
  other arithmetic  1.71 us (1%)
    ppermute x27, waiting for transfers between devices, hop(): return lax.ppermute(x, 'col', [(source, target)])  77.1 us
    ppermute x27, starting transfers between devices, hop(): return lax.ppermute(x, 'col', [(source, target)])  30.2 us
    ppermute x19, starting transfers between devices, exchange(): return lax.ppermute(x, 'scen', [(i, i ^ mask) for i in range(count)])  16.4 us
    ppermute x19, waiting for transfers between devices, exchange(): return lax.ppermute(x, 'scen', [(i, i ^ mask) for i in range(count)])  14.6 us
    unnamed x28, local copies, waits for them, and re-layouts  7.31 us
    dot_general x1, matrix products, high(): lax.dot_general(left, right, (dims, ((), ())), precision=lax.Precision.HI...  3.71 us
  transfers between devices with their start and end apart: 46, of which 22 were waited for; matrix products, arithmetic and copies ran while one was open for 3% of the time, Pallas kernels for 3%

commit v1 on v0

--- a/solution.py
+++ b/solution.py
@@ -123,75 +123,92 @@
     return one(ah, bh) + (one(ah, bl) + one(al, bh))
 
 
-def product_kernel(edges, tall, place_ref, mask_ref, inverse_hbm, coupling_hbm, *refs):
-    count = len(edges) - 1
-    pieces = refs[:count]
-    keep_a, keep_b, send, panel, rows, ph, plo, qh, ql, rect, values, sems, out_sems = refs[count:]
+def product_kernel(edges, start, stop, tall, place_ref, mask_ref, inverse_hbm, coupling_hbm, *refs):
+    given = [k for k in range(len(edges) - 1) if edges[k + 1] <= start]
+    made = [k for k in range(len(edges) - 1) if start <= edges[k] and edges[k + 1] <= stop]
+    earlier, refs = refs[: len(given)], refs[len(given) :]
+    pieces, refs = dict(zip(made, refs)), refs[len(made) :]
+    corner, (panel, rows, ph, plo, qh, ql, rect, values, sems, out_sems) = refs[:-10], refs[-10:]
 
     @pl.when(place_ref[0] == 0)
     def _():
         depth, width = panel.shape
-        nb, steps, tile = width // BLOCK, depth // tall, depth // mask_ref.shape[1]
-        copies = [pltpu.make_async_copy(coupling_hbm.at[:, pl.ds(0, width)], panel, sems.at[0])]
-        for i in range(steps):
+        nb, tile = width // BLOCK, depth // mask_ref.shape[1]
+        bring = pltpu.make_async_copy(coupling_hbm.at[:, pl.ds(0, width)], panel, sems.at[0])
+        bring.start()
+        copies = []
+        for i in range(start // tall, stop // tall):
             copies.append(pltpu.make_async_copy(inverse_hbm.at[pl.ds(i * tall, tall)], rows.at[i], sems.at[1 + i]))
-        for copy in copies:
-            copy.start()
-        stores = []
+            copies[-1].start()
+        back = []
+        for k, ref in zip(given, earlier):
+            mine = pl.ds(edges[k], edges[k + 1] - edges[k])
+            back.append(pltpu.make_async_copy(ref, values.at[mine], out_sems.at[k]))
+            back[-1].start()
         kept = [mask_ref[0, t].astype(jnp.float32) for t in range(depth // tile)]
-        copies[0].wait()
+        bring.wait()
         for t in range(depth // tile):
             here = slice(t * tile, (t + 1) * tile)
             ph[here, :], plo[here, :] = split(panel[here, :] * kept[t])
-        for i in range(steps):
-            copies[1 + i].wait()
+        stores = []
+        for i, copy in zip(range(start // tall, stop // tall), copies):
+            copy.wait()
             value = three(split(rows[i]), (ph[...], plo[...]), ((1,), (0,)))
             for t in range(i * tall // tile, (i + 1) * tall // tile):
                 part = value[t * tile - i * tall : (t + 1) * tile - i * tall, :] * kept[t]
                 here = slice(t * tile, (t + 1) * tile)
-                qh[here, :], ql[here, :] = split(part)
+                if corner:
+                    qh[here, :], ql[here, :] = split(part)
                 values[here, :] = part
-            for k in range(count):
+            for k in made:
                 if i * tall < edges[k + 1] <= (i + 1) * tall:
                     mine = pl.ds(edges[k], edges[k + 1] - edges[k])
                     stores.append(pltpu.make_async_copy(values.at[mine], pieces[k], out_sems.at[k]))
                     stores[-1].start()
-        for i, block, low in strips(nb):
-            wide = (block + 1) * BLOCK
-            mine = slice(block * BLOCK, wide)
-            rect[i * BLOCK : (i + 1) * BLOCK, low : low + wide] = three(
-                (ph[:, mine], plo[:, mine]), (qh[:, :wide], ql[:, :wide]), ((0,), (0,))
-            )
-        half = rect.shape[0] // 2
-        core = place_ref[1] & 1
-        mine = pl.multiple_of(core * half, half)
-        theirs = pl.multiple_of((1 - core) * half, half)
-        keep_a[...] = rect[pl.ds(mine, half // 2), :]
-        keep_b[...] = rect[pl.ds(mine + half // 2, half // 2), :]
-        send[...] = rect[pl.ds(theirs, half), :]
+        for k, copy in zip(given, back):
+            copy.wait()
+            here = slice(edges[k], edges[k + 1])
+            qh[here, :], ql[here, :] = split(values[here, :])
+        if corner:
+            keep_a, keep_b, send = corner
+            for i, block, low in strips(nb):
+                wide = (block + 1) * BLOCK
+                mine = slice(block * BLOCK, wide)
+                rect[i * BLOCK : (i + 1) * BLOCK, low : low + wide] = three(
+                    (ph[:, mine], plo[:, mine]), (qh[:, :wide], ql[:, :wide]), ((0,), (0,))
+                )
+            half = rect.shape[0] // 2
+            core = place_ref[1] & 1
+            mine = pl.multiple_of(core * half, half)
+            theirs = pl.multiple_of((1 - core) * half, half)
+            keep_a[...] = rect[pl.ds(mine, half // 2), :]
+            keep_b[...] = rect[pl.ds(mine + half // 2, half // 2), :]
+            send[...] = rect[pl.ds(theirs, half), :]
         for store in stores:
             store.wait()
 
 
-def product(place, mask, inverse, coupling, width, edges):
+def product(place, mask, inverse, coupling, width, edges, start, stop, earlier):
     depth, count = inverse.shape[0], len(edges) - 1
-    nb, tall = width // BLOCK, depth // 4
+    nb, tall = width // BLOCK, edges[HEAD]
     high_rows, wide = nb // 2 * BLOCK, (nb + 1) * BLOCK
+    made = [shape(b - a, width) for a, b in zip(edges, edges[1:]) if start <= a and b <= stop]
+    corner = [shape(high_rows // 4, wide), shape(high_rows // 4, wide), shape(high_rows // 2, wide)]
+    corner = corner if stop == depth else []
     return pl.pallas_call(
-        functools.partial(product_kernel, edges, tall),
-        out_shape=tuple(shape(b - a, width) for a, b in zip(edges, edges[1:]))
-        + (shape(high_rows // 4, wide), shape(high_rows // 4, wide), shape(high_rows // 2, wide)),
-        in_specs=[SMEM, SMEM, HBM, HBM],
-        out_specs=tuple([HBM] * count + vmem(3)),
+        functools.partial(product_kernel, edges, start, stop, tall),
+        out_shape=tuple(made + corner),
+        in_specs=[SMEM, SMEM, HBM, HBM] + [HBM] * len(earlier),
+        out_specs=tuple([HBM] * len(made) + vmem(len(corner))),
         scratch_shapes=[pltpu.VMEM((depth, width), jnp.float32), pltpu.VMEM((depth // tall, tall, depth), jnp.float32)]
         + [pltpu.VMEM((depth, width), jnp.bfloat16)] * 4
         + [pltpu.VMEM((high_rows, wide), jnp.float32), pltpu.VMEM((depth, width), jnp.float32)]
         + [pltpu.SemaphoreType.DMA((1 + depth // tall,)), pltpu.SemaphoreType.DMA((count,))],
         compiler_params=pltpu.CompilerParams(vmem_limit_bytes=61 << 20),
         cost_estimate=pl.CostEstimate(
-            flops=6 * depth * width * (depth + width), bytes_accessed=4 * depth * (depth + 2 * width), transcendentals=0
+            flops=6 * depth * width * (stop - start), bytes_accessed=4 * depth * (depth + 2 * width), transcendentals=0
         ),
-    )(place, mask, inverse, coupling)
+    )(place, mask, inverse, coupling, *earlier)
 
 
 def collect_kernel(planes, count, place_ref, *refs):
@@ -492,6 +509,7 @@
 
 PIECES = 8
 LATE = 1
+HEAD = 2
 
 
 def bounds(depth):
@@ -508,7 +526,10 @@
     place = jnp.stack([plane, me, plane * local.shape[1] + me * rows])
     edge = bounds(local.shape[0])
 
-    *own, keep_a, keep_b, send = product(place, tile_mask, inverses[0], local, width, edge)
+    given = (place, tile_mask, inverses[0], local, width, edge)
+    own = list(product(*given, 0, edge[HEAD], []))
+    *more, keep_a, keep_b, send = product(*given, edge[HEAD], edge[-1], own)
+    own += more
 
     groups = [own]
     for h in range(planes - 1):

time: 161 us -> 154 us (0.957)
  waiting for transfers between devices: 91.7 us -> 85.9 us
  local copies, waits for them, and re-layouts: 7.31 us -> 5.42 us
    ppermute x27, waiting for transfers between devices: 77.1 us -> 71.4 us  [hop(): return lax.ppermute(x, 'col', [(source, target)])]
    unnamed x28, local copies, waits for them, and re-layouts: 7.31 us -> 5.42 us
  transfers between devices with their start and end apart: 46 -> 46, of which waited for: 22 -> 22; matrix products, arithmetic and copies ran while one was open for 3% -> 3% of each run, Pallas kernels for 3% -> 4%
where the time goes in v1:
time: 154 us
  waiting for transfers between devices  85.9 us (56%)
  starting transfers between devices  46.9 us (30%)
  Pallas kernels  9.24 us (6%)
  local copies, waits for them, and re-layouts  5.42 us (4%)
  matrix products  3.7 us (2%)
  other arithmetic  1.75 us (1%)
    ppermute x27, waiting for transfers between devices, hop(): return lax.ppermute(x, 'col', [(source, target)])  71.4 us
    ppermute x27, starting transfers between devices, hop(): return lax.ppermute(x, 'col', [(source, target)])  30.4 us
    ppermute x19, starting transfers between devices, exchange(): return lax.ppermute(x, 'scen', [(i, i ^ mask) for i in range(count)])  16.6 us
    ppermute x19, waiting for transfers between devices, exchange(): return lax.ppermute(x, 'scen', [(i, i ^ mask) for i in range(count)])  14.5 us
    unnamed x28, local copies, waits for them, and re-layouts  5.42 us
    dot_general x1, matrix products, high(): lax.dot_general(left, right, (dims, ((), ())), precision=lax.Precision.HI...  3.7 us
  transfers between devices with their start and end apart: 46, of which 22 were waited for; matrix products, arithmetic and copies ran while one was open for 3% of the time, Pallas kernels for 4%

profile of v1, /device:TPU:16, one launch (start us, length us, event | category | flops | bytes accessed | tf_op | source)
XLA Modules:
  0.0 153.5 jit_solution(12152100810060906552)
XLA Ops:
  3.0 1.6 %shard_map.47 = (f32[128,512]{1,0:T(8,128)}, f32[128,512]{1,0:T(8,128)}, f32[128,512]{1,0:T(8,128)}, f32[128,512]{1,0:T(8,128)}, f32[128,512]{1,0:T(8,128)}, /*i...) custom-call(s32[3]{0:T(128)} %pad_add_fusion.place_ref, s32[1,8]{1,0:T(1,128)} %mask_ref.3, ...), custom_call_target="tpu_custom_call" | custom-call | flops 2415919104 | bytes 8388608 | tf_op jit(solution)/shard_map/pallas_call | solution.py:198
  15.3 22.3 %collective-permute-done.24.refs_14_ = f32[128,512]{1,0:T(8,128)S(1)} collective-permute-done((f32[128,512]{1,0:T(8,128)S(1)}, f32[128,512]{1,0:T(8,128)S(1)}, u32[]{:S(2)}, u32[]{:S(2)}) %collective-permute-start.24) | collective-permute-done | bytes 262176 | tf_op jit(solution)/shard_map/ppermute | solution.py:447
  39.0 4.3 %collective-permute-done.25.refs_15_ = f32[128,512]{1,0:T(8,128)S(1)} collective-permute-done((f32[128,512]{1,0:T(8,128)S(1)}, f32[128,512]{1,0:T(8,128)S(1)}, u32[]{:S(2)}, u32[]{:S(2)}) %collective-permute-start.25) | collective-permute-done | bytes 262176 | tf_op jit(solution)/shard_map/ppermute | solution.py:447
  44.6 4.3 %collective-permute-done.26.refs_16_ = f32[128,512]{1,0:T(8,128)S(1)} collective-permute-done((f32[128,512]{1,0:T(8,128)S(1)}, f32[128,512]{1,0:T(8,128)S(1)}, u32[]{:S(2)}, u32[]{:S(2)}) %collective-permute-start.26) | collective-permute-done | bytes 262176 | tf_op jit(solution)/shard_map/ppermute | solution.py:447
  50.2 4.3 %collective-permute-done.27.refs_17_ = f32[128,512]{1,0:T(8,128)S(1)} collective-permute-done((f32[128,512]{1,0:T(8,128)S(1)}, f32[128,512]{1,0:T(8,128)S(1)}, u32[]{:S(2)}, u32[]{:S(2)}) %collective-permute-start.27) | collective-permute-done | bytes 262176 | tf_op jit(solution)/shard_map/ppermute | solution.py:447
  55.8 5.1 %collective-permute-done.28.refs_18_ = f32[128,512]{1,0:T(8,128)S(1)} collective-permute-done((f32[128,512]{1,0:T(8,128)S(1)}, f32[128,512]{1,0:T(8,128)S(1)}, u32[]{:S(2)}, u32[]{:S(2)}) %collective-permute-start.28) | collective-permute-done | bytes 262176 | tf_op jit(solution)/shard_map/ppermute | solution.py:447
  62.2 4.3 %collective-permute-done.29.refs_19_ = f32[128,512]{1,0:T(8,128)S(1)} collective-permute-done((f32[128,512]{1,0:T(8,128)S(1)}, f32[128,512]{1,0:T(8,128)S(1)}, u32[]{:S(2)}, u32[]{:S(2)}) %collective-permute-start.29) | collective-permute-done | bytes 262176 | tf_op jit(solution)/shard_map/ppermute | solution.py:447
  67.8 4.3 %collective-permute-done.30.refs_20_ = f32[128,512]{1,0:T(8,128)S(1)} collective-permute-done((f32[128,512]{1,0:T(8,128)S(1)}, f32[128,512]{1,0:T(8,128)S(1)}, u32[]{:S(2)}, u32[]{:S(2)}) %collective-permute-start.30) | collective-permute-done | bytes 262176 | tf_op jit(solution)/shard_map/ppermute | solution.py:447
  73.5 3.5 %collective-permute-done.39.refs_2_ = f32[128,512]{1,0:T(8,128)S(1)} collective-permute-done((f32[128,512]{1,0:T(8,128)S(1)}, f32[128,512]{1,0:T(8,128)S(1)}, u32[]{:S(2)}, u32[]{:S(2)}) %collective-permute-start.39) | collective-permute-done | bytes 262176 | tf_op jit(solution)/shard_map/ppermute | solution.py:447
  81.1 1.6 %collective-permute-start.40 = (f32[128,512]{1,0:T(8,128)S(1)}, f32[128,512]{1,0:T(8,128)S(1)}, u32[]{:S(2)}, u32[]{:S(2)}) collective-permute-start(f32[128,512]{1,0:T(8,128)S(1)} %collective-permute-done.39.refs_2_), channel_id=1, source_target_pairs={{2,3},{6,7},{10,11},{14,15},{18,19},{22,23},{26,27},{30,31}} | collective-permute-start | bytes 786440 | tf_op jit(solution)/shard_map/ppermute | solution.py:447
  82.6 2.3 %collective-permute-done.35.refs_25_ = f32[128,512]{1,0:T(8,128)S(1)} collective-permute-done((f32[128,512]{1,0:T(8,128)S(1)}, f32[128,512]{1,0:T(8,128)S(1)}, u32[]{:S(2)}, u32[]{:S(2)}) %collective-permute-start.35) | collective-permute-done | bytes 262176 | tf_op jit(solution)/shard_map/ppermute | solution.py:447
  85.0 5.6 %collective-permute-done.36.refs_26_ = f32[128,512]{1,0:T(8,128)S(1)} collective-permute-done((f32[128,512]{1,0:T(8,128)S(1)}, f32[128,512]{1,0:T(8,128)S(1)}, u32[]{:S(2)}, u32[]{:S(2)}) %collective-permute-start.36) | collective-permute-done | bytes 262176 | tf_op jit(solution)/shard_map/ppermute | solution.py:447
  90.6 5.6 %collective-permute-done.37.refs_27_ = f32[128,512]{1,0:T(8,128)S(1)} collective-permute-done((f32[128,512]{1,0:T(8,128)S(1)}, f32[128,512]{1,0:T(8,128)S(1)}, u32[]{:S(2)}, u32[]{:S(2)}) %collective-permute-start.37) | collective-permute-done | bytes 262176 | tf_op jit(solution)/shard_map/ppermute | solution.py:447
  101.8 3.7 %fusion.first_ref = f32[512,1024]{1,0:T(8,128)S(1)} fusion(f32[896,512]{1,0:T(8,128)S(1)} %shard_map.49, f32[1,1024,1024]{2,1,0:T(8,128)S(1)} %copy-done), kind=kOutput, calls=%fused_computation | convolution fusion | flops 2818572288 | bytes 7602176 | tf_op jit(solution)/shard_map/dot_general | solution.py:16
  105.5 1.7 %shard_map.50 = (f32[4,512,128]{2,1,0:T(8,128)S(1)}, f32[4,512,128]{2,1,0:T(8,128)S(1)}) custom-call(s32[3]{0:T(128)S(1)} %copy-done.9, f32[512,1024]{1,0:T(8,128)S(1)} %fusion.first_ref, f32[1024,1024]{1,0:T(8,128)S(1)} %bitcast.12, f32[128,512]{1,0:T(8,128)S(1)} %copy-done.8, f32[128,512]{1,0:T(8,128)S(1)} %collective-permute-done.38.refs_1_, ...), custom_call_target="tpu_custom_call" | custom-call | flops 402653184 | bytes 4194304 | tf_op jit(solution)/shard_map/pallas_call | solution.py:272
  107.4 1.7 %collective-permute-start.3 = (f32[64,640]{1,0:T(8,128)S(1)}, f32[64,640]{1,0:T(8,128)S(1)}, u32[]{:S(2)}, u32[]{:S(2)}) collective-permute-start(f32[64,640]{1,0:T(8,128)S(1)} %get-tuple-element.51), channel_id=1, source_target_pairs={{0,16},{4,20},{8,24},{12,28},{16,0},{20,4},{24,8},{28,12},{1,17},{... | collective-permute-start | bytes 491528 | tf_op jit(solution)/shard_map/ppermute | solution.py:451
  109.1 1.5 collective-permute-start.1
  110.6 3.4 %collective-permute-done.3 = f32[64,640]{1,0:T(8,128)S(1)} collective-permute-done((f32[64,640]{1,0:T(8,128)S(1)}, f32[64,640]{1,0:T(8,128)S(1)}, u32[]{:S(2)}, u32[]{:S(2)}) %collective-permute-start.3) | collective-permute-done | bytes 163872 | tf_op jit(solution)/shard_map/ppermute | solution.py:451
  114.0 1.7 %collective-permute-start.4 = (f32[64,640]{1,0:T(8,128)S(1)}, f32[64,640]{1,0:T(8,128)S(1)}, u32[]{:S(2)}, u32[]{:S(2)}) collective-permute-start(f32[64,640]{1,0:T(8,128)S(1)} %add.35), channel_id=1, source_target_pairs={{0,8},{4,12},{8,0},{12,4},{16,24},{20,28},{24,16},{28,20},{1,9},{5... | collective-permute-start | bytes 491528 | tf_op jit(solution)/shard_map/ppermute | solution.py:451
  115.7 1.6 %collective-permute-start.2 = (f32[64,640]{1,0:T(8,128)S(1)}, f32[64,640]{1,0:T(8,128)S(1)}, u32[]{:S(2)}, u32[]{:S(2)}) collective-permute-start(f32[64,640]{1,0:T(8,128)S(1)} %add.32), channel_id=1, source_target_pairs={{0,16},{4,20},{8,24},{12,28},{16,0},{20,4},{24,8},{28,12},{1,17},{... | collective-permute-start | bytes 491528 | tf_op jit(solution)/shard_map/ppermute | solution.py:451
  117.4 2.5 %collective-permute-done.4 = f32[64,640]{1,0:T(8,128)S(1)} collective-permute-done((f32[64,640]{1,0:T(8,128)S(1)}, f32[64,640]{1,0:T(8,128)S(1)}, u32[]{:S(2)}, u32[]{:S(2)}) %collective-permute-start.4) | collective-permute-done | bytes 163872 | tf_op jit(solution)/shard_map/ppermute | solution.py:451
  119.9 1.3 collective-permute-done.2
  121.4 1.4 collective-permute-done.5.other_a
  126.1 5.2 %collective-permute-done.8 = f32[32,640]{1,0:T(8,128)} collective-permute-done((f32[32,640]{1,0:T(8,128)S(1)}, f32[32,640]{1,0:T(8,128)}, u32[]{:S(2)}, u32[]{:S(2)}) %collective-permute-start.8) | collective-permute-done | bytes 81952 | tf_op jit(solution)/shard_map/ppermute | solution.py:447
  131.3 1.9 %collective-permute-start.9 = (f32[32,640]{1,0:T(8,128)}, f32[32,640]{1,0:T(8,128)}, u32[]{:S(2)}, u32[]{:S(2)}) collective-permute-start(f32[32,640]{1,0:T(8,128)} %collective-permute-done.8), channel_id=1, source_target_pairs={{2,3},{6,7},{10,11},{14,15},{18,19},{22,23},{26,27},{30,31}} | collective-permute-start | bytes 245768 | tf_op jit(solution)/shard_map/ppermute | solution.py:447
  137.2 1.3 collective-permute-start.15
  138.5 1.6 %collective-permute-start.13 = (f32[32,640]{1,0:T(8,128)S(1)}, f32[32,640]{1,0:T(8,128)S(1)}, u32[]{:S(2)}, u32[]{:S(2)}) collective-permute-start(f32[32,640]{1,0:T(8,128)S(1)} %add_add_fusion.refs_0_), channel_id=1, source_target_pairs={{0,16},{4,20},{8,24},{12,28},{16,0},{20,4},{24,8},{28,12},{1,17},{... | collective-permute-start | bytes 245768 | tf_op jit(solution)/shard_map/ppermute | solution.py:451
  140.7 2.4 %collective-permute-done.42.got_ref = f32[2,256,128]{2,1,0:T(8,128)S(1)} collective-permute-done((f32[2,256,128]{2,1,0:T(8,128)S(1)}, f32[2,256,128]{2,1,0:T(8,128)S(1)}, u32[]{:S(2)}, u32[]{:S(2)}) %collective-permute-start.42) | collective-permute-done | bytes 262176 | tf_op jit(solution)/shard_map/ppermute | solution.py:451
  144.1 2.0 %collective-permute-start.43 = (f32[1,256,128]{2,1,0:T(8,128)S(1)}, f32[1,256,128]{2,1,0:T(8,128)S(1)}, u32[]{:S(2)}, u32[]{:S(2)}) collective-permute-start(f32[1,256,128]{2,1,0:T(8,128)S(1)} %get-tuple-element.45), channel_id=1, source_target_pairs={{0,16},{4,20},{8,24},{12,28},{16,0},{20,4},{24,8},{28,12},{1,17},{... | collective-permute-start | bytes 393224 | tf_op jit(solution)/shard_map/ppermute | solution.py:451
  146.7 1.3 collective-permute-start.45
  149.9 1.9 %collective-permute-done.45.refs_11_ = f32[1,256,128]{2,1,0:T(8,128)S(1)} collective-permute-done((f32[1,256,128]{2,1,0:T(8,128)S(1)}, f32[1,256,128]{2,1,0:T(8,128)S(1)}, u32[]{:S(2)}, u32[]{:S(2)}) %collective-permute-start.45) | collective-permute-done | bytes 131104 | tf_op jit(solution)/shard_map/ppermute | solution.py:451
  151.8 1.8 %shard_map.54 = f32[128,512]{1,0:T(8,128)} custom-call(s32[3]{0:T(128)S(1)} %copy-done.9, f32[32,640]{1,0:T(8,128)S(1)} %add_add_fusion.refs_0_, f32[32,640]{1,0:T(8,128)S(1)} %collective-permute-done.10.refs_1_, f32[32,640]{1,0:T(8,128)S(1)} %collective-permute-done.11.refs_2_, f32[32,640]{1,0:T(8,128)S(1)} %collective-permute-done.12.refs_3_, ...), custom_call_target="tpu_custom_call" | custom-call | flops 201326592 | bytes 2097152 | tf_op jit(solution)/shard_map/pallas_call | solution.py:435
  (105 shorter events, 43.6 us)
Async XLA Ops:
  7.4 5.3 %collective-permute-start.23 = (f32[128,512]{1,0:T(8,128)}, f32[128,512]{1,0:T(8,128)S(1)}, u32[]{:S(2)}, u32[]{:S(2)}) collective-permute-start(f32[128,512]{1,0:T(8,128)} %get-tuple-element.38.refs_6_), channel_id=1, source_target_pairs={{0,1},{4,5},{8,9},{12,13},{16,17},{20,21},{24,25},{28,29}} | collective-permute-start | bytes 786440 | tf_op jit(solution)/shard_map/ppermute | solution.py:447
  8.1 5.9 %collective-permute-start.38 = (f32[128,512]{1,0:T(8,128)}, f32[128,512]{1,0:T(8,128)S(1)}, u32[]{:S(2)}, u32[]{:S(2)}) collective-permute-start(f32[128,512]{1,0:T(8,128)} %get-tuple-element.39.refs_0_), channel_id=1, source_target_pairs={{0,1},{4,5},{8,9},{12,13},{16,17},{20,21},{24,25},{28,29}} | collective-permute-start | bytes 786440 | tf_op jit(solution)/shard_map/ppermute | solution.py:447
  8.8 28.9 %collective-permute-start.24 = (f32[128,512]{1,0:T(8,128)S(1)}, f32[128,512]{1,0:T(8,128)S(1)}, u32[]{:S(2)}, u32[]{:S(2)}) collective-permute-start(f32[128,512]{1,0:T(8,128)S(1)} %collective-permute-done.17.refs_7_), channel_id=1, source_target_pairs={{1,2},{5,6},{9,10},{13,14},{17,18},{21,22},{25,26},{29,30}} | collective-permute-start | bytes 786440 | tf_op jit(solution)/shard_map/ppermute | solution.py:447
  10.1 33.2 %collective-permute-start.25 = (f32[128,512]{1,0:T(8,128)S(1)}, f32[128,512]{1,0:T(8,128)S(1)}, u32[]{:S(2)}, u32[]{:S(2)}) collective-permute-start(f32[128,512]{1,0:T(8,128)S(1)} %collective-permute-done.18.refs_8_), channel_id=1, source_target_pairs={{1,2},{5,6},{9,10},{13,14},{17,18},{21,22},{25,26},{29,30}} | collective-permute-start | bytes 786440 | tf_op jit(solution)/shard_map/ppermute | solution.py:447
  11.4 37.5 %collective-permute-start.26 = (f32[128,512]{1,0:T(8,128)S(1)}, f32[128,512]{1,0:T(8,128)S(1)}, u32[]{:S(2)}, u32[]{:S(2)}) collective-permute-start(f32[128,512]{1,0:T(8,128)S(1)} %collective-permute-done.19.refs_9_), channel_id=1, source_target_pairs={{1,2},{5,6},{9,10},{13,14},{17,18},{21,22},{25,26},{29,30}} | collective-permute-start | bytes 786440 | tf_op jit(solution)/shard_map/ppermute | solution.py:447
  12.7 41.8 %collective-permute-start.27 = (f32[128,512]{1,0:T(8,128)S(1)}, f32[128,512]{1,0:T(8,128)S(1)}, u32[]{:S(2)}, u32[]{:S(2)}) collective-permute-start(f32[128,512]{1,0:T(8,128)S(1)} %collective-permute-done.20.refs_10_), channel_id=1, source_target_pairs={{1,2},{5,6},{9,10},{13,14},{17,18},{21,22},{25,26},{29,30}} | collective-permute-start | bytes 786440 | tf_op jit(solution)/shard_map/ppermute | solution.py:447
  14.0 46.9 %collective-permute-start.28 = (f32[128,512]{1,0:T(8,128)S(1)}, f32[128,512]{1,0:T(8,128)S(1)}, u32[]{:S(2)}, u32[]{:S(2)}) collective-permute-start(f32[128,512]{1,0:T(8,128)S(1)} %collective-permute-done.21.refs_11_), channel_id=1, source_target_pairs={{1,2},{5,6},{9,10},{13,14},{17,18},{21,22},{25,26},{29,30}} | collective-permute-start | bytes 786440 | tf_op jit(solution)/shard_map/ppermute | solution.py:447
  37.7 28.9 %collective-permute-start.29 = (f32[128,512]{1,0:T(8,128)S(1)}, f32[128,512]{1,0:T(8,128)S(1)}, u32[]{:S(2)}, u32[]{:S(2)}) collective-permute-start(f32[128,512]{1,0:T(8,128)S(1)} %collective-permute-done.22.refs_12_), channel_id=1, source_target_pairs={{1,2},{5,6},{9,10},{13,14},{17,18},{21,22},{25,26},{29,30}} | collective-permute-start | bytes 786440 | tf_op jit(solution)/shard_map/ppermute | solution.py:447
  43.3 28.9 %collective-permute-start.30 = (f32[128,512]{1,0:T(8,128)S(1)}, f32[128,512]{1,0:T(8,128)S(1)}, u32[]{:S(2)}, u32[]{:S(2)}) collective-permute-start(f32[128,512]{1,0:T(8,128)S(1)} %collective-permute-done.23.refs_13_), channel_id=1, source_target_pairs={{1,2},{5,6},{9,10},{13,14},{17,18},{21,22},{25,26},{29,30}} | collective-permute-start | bytes 786440 | tf_op jit(solution)/shard_map/ppermute | solution.py:447
  48.9 28.1 %collective-permute-start.39 = (f32[128,512]{1,0:T(8,128)S(1)}, f32[128,512]{1,0:T(8,128)S(1)}, u32[]{:S(2)}, u32[]{:S(2)}) collective-permute-start(f32[128,512]{1,0:T(8,128)S(1)} %collective-permute-done.38.refs_1_), channel_id=1, source_target_pairs={{1,2},{5,6},{9,10},{13,14},{17,18},{21,22},{25,26},{29,30}} | collective-permute-start | bytes 786440 | tf_op jit(solution)/shard_map/ppermute | solution.py:447
  54.5 23.8 %collective-permute-start.31 = (f32[128,512]{1,0:T(8,128)S(1)}, f32[128,512]{1,0:T(8,128)S(1)}, u32[]{:S(2)}, u32[]{:S(2)}) collective-permute-start(f32[128,512]{1,0:T(8,128)S(1)} %collective-permute-done.24.refs_14_), channel_id=1, source_target_pairs={{2,3},{6,7},{10,11},{14,15},{18,19},{22,23},{26,27},{30,31}} | collective-permute-start | bytes 786440 | tf_op jit(solution)/shard_map/ppermute | solution.py:447
  60.9 18.7 %collective-permute-start.32 = (f32[128,512]{1,0:T(8,128)S(1)}, f32[128,512]{1,0:T(8,128)S(1)}, u32[]{:S(2)}, u32[]{:S(2)}) collective-permute-start(f32[128,512]{1,0:T(8,128)S(1)} %collective-permute-done.25.refs_15_), channel_id=1, source_target_pairs={{2,3},{6,7},{10,11},{14,15},{18,19},{22,23},{26,27},{30,31}} | collective-permute-start | bytes 786440 | tf_op jit(solution)/shard_map/ppermute | solution.py:447
  66.5 14.4 %collective-permute-start.33 = (f32[128,512]{1,0:T(8,128)S(1)}, f32[128,512]{1,0:T(8,128)S(1)}, u32[]{:S(2)}, u32[]{:S(2)}) collective-permute-start(f32[128,512]{1,0:T(8,128)S(1)} %collective-permute-done.26.refs_16_), channel_id=1, source_target_pairs={{2,3},{6,7},{10,11},{14,15},{18,19},{22,23},{26,27},{30,31}} | collective-permute-start | bytes 786440 | tf_op jit(solution)/shard_map/ppermute | solution.py:447
  72.2 8.9 %collective-permute-start.34 = (f32[128,512]{1,0:T(8,128)S(1)}, f32[128,512]{1,0:T(8,128)S(1)}, u32[]{:S(2)}, u32[]{:S(2)}) collective-permute-start(f32[128,512]{1,0:T(8,128)S(1)} %collective-permute-done.27.refs_17_), channel_id=1, source_target_pairs={{2,3},{6,7},{10,11},{14,15},{18,19},{22,23},{26,27},{30,31}} | collective-permute-start | bytes 786440 | tf_op jit(solution)/shard_map/ppermute | solution.py:447
  77.0 8.0 %collective-permute-start.35 = (f32[128,512]{1,0:T(8,128)S(1)}, f32[128,512]{1,0:T(8,128)S(1)}, u32[]{:S(2)}, u32[]{:S(2)}) collective-permute-start(f32[128,512]{1,0:T(8,128)S(1)} %collective-permute-done.28.refs_18_), channel_id=1, source_target_pairs={{2,3},{6,7},{10,11},{14,15},{18,19},{22,23},{26,27},{30,31}} | collective-permute-start | bytes 786440 | tf_op jit(solution)/shard_map/ppermute | solution.py:447
  78.3 12.3 %collective-permute-start.36 = (f32[128,512]{1,0:T(8,128)S(1)}, f32[128,512]{1,0:T(8,128)S(1)}, u32[]{:S(2)}, u32[]{:S(2)}) collective-permute-start(f32[128,512]{1,0:T(8,128)S(1)} %collective-permute-done.29.refs_19_), channel_id=1, source_target_pairs={{2,3},{6,7},{10,11},{14,15},{18,19},{22,23},{26,27},{30,31}} | collective-permute-start | bytes 786440 | tf_op jit(solution)/shard_map/ppermute | solution.py:447
  79.6 16.6 %collective-permute-start.37 = (f32[128,512]{1,0:T(8,128)S(1)}, f32[128,512]{1,0:T(8,128)S(1)}, u32[]{:S(2)}, u32[]{:S(2)}) collective-permute-start(f32[128,512]{1,0:T(8,128)S(1)} %collective-permute-done.30.refs_20_), channel_id=1, source_target_pairs={{2,3},{6,7},{10,11},{14,15},{18,19},{22,23},{26,27},{30,31}} | collective-permute-start | bytes 786440 | tf_op jit(solution)/shard_map/ppermute | solution.py:447
  81.0 26.3 %collective-permute-start = (f32[128,640]{1,0:T(8,128)}, f32[128,640]{1,0:T(8,128)S(1)}, u32[]{:S(2)}, u32[]{:S(2)}) collective-permute-start(f32[128,640]{1,0:T(8,128)} %get-tuple-element.31), channel_id=1, source_target_pairs={{0,4},{4,0},{8,12},{12,8},{16,20},{20,16},{24,28},{28,24},{1,5},{5... | collective-permute-start | bytes 983048 | tf_op jit(solution)/shard_map/ppermute | solution.py:451
  81.1 24.4 %collective-permute-start.40 = (f32[128,512]{1,0:T(8,128)S(1)}, f32[128,512]{1,0:T(8,128)S(1)}, u32[]{:S(2)}, u32[]{:S(2)}) collective-permute-start(f32[128,512]{1,0:T(8,128)S(1)} %collective-permute-done.39.refs_2_), channel_id=1, source_target_pairs={{2,3},{6,7},{10,11},{14,15},{18,19},{22,23},{26,27},{30,31}} | collective-permute-start | bytes 786440 | tf_op jit(solution)/shard_map/ppermute | solution.py:447
  107.2 26.0 %collective-permute-start.41 = (f32[4,512,128]{2,1,0:T(8,128)S(1)}, f32[4,512,128]{2,1,0:T(8,128)S(1)}, u32[]{:S(2)}, u32[]{:S(2)}) collective-permute-start(f32[4,512,128]{2,1,0:T(8,128)S(1)} %get-tuple-element.41), channel_id=1, source_target_pairs={{0,4},{4,0},{8,12},{12,8},{16,20},{20,16},{24,28},{28,24},{1,5},{5... | collective-permute-start | bytes 3145736 | tf_op jit(solution)/shard_map/ppermute | solution.py:451
  107.4 6.6 %collective-permute-start.3 = (f32[64,640]{1,0:T(8,128)S(1)}, f32[64,640]{1,0:T(8,128)S(1)}, u32[]{:S(2)}, u32[]{:S(2)}) collective-permute-start(f32[64,640]{1,0:T(8,128)S(1)} %get-tuple-element.51), channel_id=1, source_target_pairs={{0,16},{4,20},{8,24},{12,28},{16,0},{20,4},{24,8},{28,12},{1,17},{... | collective-permute-start | bytes 491528 | tf_op jit(solution)/shard_map/ppermute | solution.py:451
  109.1 6.6 %collective-permute-start.1 = (f32[64,640]{1,0:T(8,128)S(1)}, f32[64,640]{1,0:T(8,128)S(1)}, u32[]{:S(2)}, u32[]{:S(2)}) collective-permute-start(f32[64,640]{1,0:T(8,128)S(1)} %get-tuple-element.52), channel_id=1, source_target_pairs={{0,8},{4,12},{8,0},{12,4},{16,24},{20,28},{24,16},{28,20},{1,9},{5... | collective-permute-start | bytes 491528 | tf_op jit(solution)/shard_map/ppermute | solution.py:451
  114.0 5.8 %collective-permute-start.4 = (f32[64,640]{1,0:T(8,128)S(1)}, f32[64,640]{1,0:T(8,128)S(1)}, u32[]{:S(2)}, u32[]{:S(2)}) collective-permute-start(f32[64,640]{1,0:T(8,128)S(1)} %add.35), channel_id=1, source_target_pairs={{0,8},{4,12},{8,0},{12,4},{16,24},{20,28},{24,16},{28,20},{1,9},{5... | collective-permute-start | bytes 491528 | tf_op jit(solution)/shard_map/ppermute | solution.py:451
  115.7 5.5 %collective-permute-start.2 = (f32[64,640]{1,0:T(8,128)S(1)}, f32[64,640]{1,0:T(8,128)S(1)}, u32[]{:S(2)}, u32[]{:S(2)}) collective-permute-start(f32[64,640]{1,0:T(8,128)S(1)} %add.32), channel_id=1, source_target_pairs={{0,16},{4,20},{8,24},{12,28},{16,0},{20,4},{24,8},{28,12},{1,17},{... | collective-permute-start | bytes 491528 | tf_op jit(solution)/shard_map/ppermute | solution.py:451
  124.8 6.5 %collective-permute-start.8 = (f32[32,640]{1,0:T(8,128)S(1)}, f32[32,640]{1,0:T(8,128)}, u32[]{:S(2)}, u32[]{:S(2)}) collective-permute-start(f32[32,640]{1,0:T(8,128)S(1)} %collective-permute-done.7), channel_id=1, source_target_pairs={{1,2},{5,6},{9,10},{13,14},{17,18},{21,22},{25,26},{29,30}} | collective-permute-start | bytes 245768 | tf_op jit(solution)/shard_map/ppermute | solution.py:447
  133.9 9.2 %collective-permute-start.42 = (f32[2,256,128]{2,1,0:T(8,128)S(1)}, f32[2,256,128]{2,1,0:T(8,128)S(1)}, u32[]{:S(2)}, u32[]{:S(2)}) collective-permute-start(f32[2,256,128]{2,1,0:T(8,128)S(1)} %get-tuple-element.43), channel_id=1, source_target_pairs={{0,8},{4,12},{8,0},{12,4},{16,24},{20,28},{24,16},{28,20},{1,9},{5... | collective-permute-start | bytes 786440 | tf_op jit(solution)/shard_map/ppermute | solution.py:451
  135.1 9.0 %collective-permute-start.44 = (f32[2,256,128]{2,1,0:T(8,128)S(1)}, f32[2,256,128]{2,1,0:T(8,128)S(1)}, u32[]{:S(2)}, u32[]{:S(2)}) collective-permute-start(f32[2,256,128]{2,1,0:T(8,128)S(1)} %get-tuple-element.47), channel_id=1, source_target_pairs={{0,16},{4,20},{8,24},{12,28},{16,0},{20,4},{24,8},{28,12},{1,17},{... | collective-permute-start | bytes 786440 | tf_op jit(solution)/shard_map/ppermute | solution.py:451
  137.2 9.6 %collective-permute-start.15 = (f32[32,640]{1,0:T(8,128)S(1)}, f32[32,640]{1,0:T(8,128)S(1)}, u32[]{:S(2)}, u32[]{:S(2)}) collective-permute-start(f32[32,640]{1,0:T(8,128)S(1)} %add_add_fusion.refs_0_), channel_id=1, source_target_pairs={{0,24},{4,28},{8,16},{12,20},{16,8},{20,12},{24,0},{28,4},{1,25},{... | collective-permute-start | bytes 245768 | tf_op jit(solution)/shard_map/ppermute | solution.py:451
  138.5 9.5 %collective-permute-start.13 = (f32[32,640]{1,0:T(8,128)S(1)}, f32[32,640]{1,0:T(8,128)S(1)}, u32[]{:S(2)}, u32[]{:S(2)}) collective-permute-start(f32[32,640]{1,0:T(8,128)S(1)} %add_add_fusion.refs_0_), channel_id=1, source_target_pairs={{0,16},{4,20},{8,24},{12,28},{16,0},{20,4},{24,8},{28,12},{1,17},{... | collective-permute-start | bytes 245768 | tf_op jit(solution)/shard_map/ppermute | solution.py:451
  140.1 8.0 %collective-permute-start.11 = (f32[32,640]{1,0:T(8,128)S(1)}, f32[32,640]{1,0:T(8,128)S(1)}, u32[]{:S(2)}, u32[]{:S(2)}) collective-permute-start(f32[32,640]{1,0:T(8,128)S(1)} %add_add_fusion.refs_0_), channel_id=1, source_target_pairs={{0,8},{4,12},{8,0},{12,4},{16,24},{20,28},{24,16},{28,20},{1,9},{5... | collective-permute-start | bytes 245768 | tf_op jit(solution)/shard_map/ppermute | solution.py:451
  143.1 5.4 %collective-permute-start.10 = (f32[32,640]{1,0:T(8,128)S(1)}, f32[32,640]{1,0:T(8,128)S(1)}, u32[]{:S(2)}, u32[]{:S(2)}) collective-permute-start(f32[32,640]{1,0:T(8,128)S(1)} %add_add_fusion.refs_0_), channel_id=1, source_target_pairs={{0,4},{4,0},{8,12},{12,8},{16,20},{20,16},{24,28},{28,24},{1,5},{5... | collective-permute-start | bytes 245768 | tf_op jit(solution)/shard_map/ppermute | solution.py:451
  144.1 5.7 %collective-permute-start.43 = (f32[1,256,128]{2,1,0:T(8,128)S(1)}, f32[1,256,128]{2,1,0:T(8,128)S(1)}, u32[]{:S(2)}, u32[]{:S(2)}) collective-permute-start(f32[1,256,128]{2,1,0:T(8,128)S(1)} %get-tuple-element.45), channel_id=1, source_target_pairs={{0,16},{4,20},{8,24},{12,28},{16,0},{20,4},{24,8},{28,12},{1,17},{... | collective-permute-start | bytes 393224 | tf_op jit(solution)/shard_map/ppermute | solution.py:451
  (28 other events, 376.7 us)
